TPU v7x, 128 devices: a whole 4x4x4 slice. The times are simulated.
128 devices in a mesh: seq: 32 (over y, z, core), chan: 4 (over x).
Axes of the slice: x: 4, y: 4, z: 4, core: 2. Of those that a mesh axis runs over, the one named last changes fastest.
Arguments:
- tokens: bfloat16 [4, 8192, 1024], P(None, 'seq', 'chan'), may hold values from -6 to 6
- routing: int32 [8192, 4], P(('seq', 'chan')), may hold values from 0 to 31, as said below
- expert_in: bfloat16 [32, 1024, 4096], P('seq'), may hold values from -0.1875 to 0.1875
- expert_out: bfloat16 [32, 4096, 1024], P('seq'), may hold values from -0.09375 to 0.09375
- gain_mix: float32 [1024], replicated, may hold values from 0.5 to 1.5
- gain_out: float32 [1024], replicated, may hold values from 0.5 to 1.5
Outputs:
- layer_out: bfloat16 [4, 8192, 1024], P(None, ('seq', 'chan'))
Inputs may be any that keep to these rules, and one draw needn't show every extreme that they name: Read routing in the order of its flattened index (position, then document). In each aligned block of 256 entries (the tokens of one device along seq+chan) no expert appears more than 24 times, and one expert appears exactly 24 times in every block.
All inputs are finite; a program needn't handle non-finite values.
Results may differ from a plain program's by a relative error of at most 0.0095.
Values may be sent and summed in bfloat16 or wider, within the bound.
No kernel may reach another device: no remote copies, remote signals or barrier semaphores. Data moves between devices by JAX's collectives and lax.ppermute only.
A program may use at most 128 MiB of HBM per device.

v0:
```python
import math

import jax
import jax.numpy as jnp
from jax import lax
from jax.sharding import Mesh
from jax.sharding import PartitionSpec as P

SEQ = ("seq_0", "seq_1", "seq_2")
SEQ_CHAN = ("seq_0", "seq_1", "seq_2", "chan")


def joined_along(parts, dim):
    parts = jnp.moveaxis(parts, 0, dim)
    dims = parts.shape
    return parts.reshape(*dims[:dim], dims[dim] * dims[dim + 1], *dims[dim + 2 :])


def sent_to_all(x, axis):
    copies = jnp.broadcast_to(x, (lax.axis_size(axis), *x.shape))
    return lax.all_to_all(copies, axis, split_axis=0, concat_axis=0, tiled=True)


def gather_directly(x, axis, dim):
    return joined_along(sent_to_all(x, axis), dim)


def in_blocks(x, dim, size):
    dims = x.shape
    parts = x.reshape(*dims[:dim], size, dims[dim] // size, *dims[dim + 1 :])
    return jnp.moveaxis(parts, dim, 0)


def exchange_in_order(parts, axes, order):
    dims = [lax.axis_size(a) for a in axes]
    parts = parts.reshape(*dims, *parts.shape[1:])
    for k in order:
        parts = lax.all_to_all(parts, axes[k], split_axis=k, concat_axis=k, tiled=True)
    return parts.reshape(-1, *parts.shape[len(axes) :])


def two_step_exchange(x, groups, order, split_dim, concat_dim):
    size = lax.axis_size(groups[0]) * lax.axis_size(groups[1])
    parts = in_blocks(x, split_dim, size)
    return joined_along(exchange_in_order(parts, groups, order), concat_dim)


def exchange_both(x, axis, axes, splits, concats):
    sizes = [lax.axis_size(a) for a in axes]
    parts = in_blocks(x, splits[0], sizes[0])
    parts = jnp.moveaxis(in_blocks(parts, splits[1] + 1, sizes[1]), 0, 1)
    inside = parts.shape[2:]
    parts = parts.reshape(-1, *inside)
    parts = lax.all_to_all(parts, axis, split_axis=0, concat_axis=0, tiled=True)
    parts = joined_along(parts.reshape(*sizes, *inside), concats[0] + 1)
    return joined_along(parts, concats[1])


def hidden_table(freq_list, full_width):
    inputs = jnp.arange(full_width, dtype=jnp.int32)
    product = freq_list[:, None] * inputs[None, :] % full_width
    angles = product.astype(jnp.float32) * (2.0 * math.pi / full_width)
    factor = 1.0 / math.sqrt(full_width)
    return jnp.concatenate([jnp.cos(angles) * factor, -jnp.sin(angles) * factor], axis=0).astype(
        jnp.bfloat16
    )


def layer_norm(values, gain_vec):
    center = values - jnp.mean(values, axis=-1, keepdims=True)
    spread = jnp.mean(center * center, axis=-1, keepdims=True)
    return center * lax.rsqrt(spread + 1e-05) * gain_vec


def settle(values):
    return lax.optimization_barrier(values)


def split_table(table):
    upper = table.astype(jnp.bfloat16)
    lower = (table - upper.astype(jnp.float32)).astype(jnp.bfloat16)
    return (upper, lower)


def outer_apply(table, grid):
    upper, lower = split_table(table)
    first = jnp.einsum("kr,grq->gkq", upper, grid, preferred_element_type=jnp.float32)
    return first + jnp.einsum("kr,grq->gkq", lower, grid, preferred_element_type=jnp.float32)


def sequence_real(real_part, imag_part):
    groups, seq_len = real_part.shape
    inner_len = 128
    outer_len = seq_len // inner_len
    better = lax.Precision.HIGH
    outer_idx = jnp.arange(outer_len, dtype=jnp.int32)
    inner_idx = jnp.arange(inner_len, dtype=jnp.int32)
    outer_angle = (outer_idx[:, None] * outer_idx[None, :] % outer_len).astype(jnp.float32) * (
        2.0 * math.pi / outer_len
    )
    twist_angle = (outer_idx[:, None] * inner_idx[None, :] % seq_len).astype(jnp.float32) * (
        2.0 * math.pi / seq_len
    )
    inner_angle = (inner_idx[:, None] * inner_idx[None, :] % inner_len).astype(jnp.float32) * (
        2.0 * math.pi / inner_len
    )
    outer_cos = jnp.cos(outer_angle)
    outer_sin = jnp.sin(outer_angle)
    twist_cos = jnp.cos(twist_angle)
    twist_sin = jnp.sin(twist_angle)
    inner_cos = jnp.cos(inner_angle)
    inner_sin = jnp.sin(inner_angle)
    real_grid = real_part.reshape(groups, outer_len, inner_len)
    imag_grid = imag_part.reshape(groups, outer_len, inner_len)
    first_real = outer_apply(outer_cos, real_grid) + outer_apply(outer_sin, imag_grid)
    first_imag = outer_apply(outer_cos, imag_grid) - outer_apply(outer_sin, real_grid)
    second_real = first_real * twist_cos + first_imag * twist_sin
    second_imag = first_imag * twist_cos - first_real * twist_sin
    result = jnp.einsum("gkq,qm->gkm", second_real, inner_cos, precision=better) + jnp.einsum(
        "gkq,qm->gkm", second_imag, inner_sin, precision=better
    )
    return jnp.transpose(result, (0, 2, 1)).reshape(groups, seq_len) * (1.0 / math.sqrt(seq_len))


def local(tokens, routing, expert_in, expert_out, gain_mix, gain_out):
    n_seq = lax.axis_size(SEQ)
    n_chan = lax.axis_size("chan")
    chan_pos = lax.axis_index("chan")
    doc_count, pos_count, chan_width = tokens.shape
    full_width = chan_width * n_chan
    quarter = pos_count // n_chan
    narrow = full_width // (n_seq * n_chan)
    row_count = doc_count * quarter
    full_rows = gather_directly(tokens, "chan", 2)
    freq_list = chan_pos * chan_width + jnp.arange(chan_width, dtype=jnp.int32)
    dft_table = hidden_table(freq_list, full_width)
    rows_all = full_rows.reshape(doc_count * pos_count, full_width)
    spectrum = lax.dot_general(
        dft_table, rows_all, (((1,), (1,)), ((), ())), preferred_element_type=jnp.float32
    ).astype(jnp.bfloat16)
    spectrum = spectrum.reshape(2, chan_width, doc_count, pos_count)
    columns = two_step_exchange(spectrum, (("seq_0", "seq_1"), "seq_2"), (1, 0), 1, 3)
    residual = lax.dynamic_slice_in_dim(full_rows, chan_pos * quarter, quarter, 1)
    seq_len = columns.shape[3]
    mixing = sequence_real(
        columns[0].reshape(narrow * doc_count, seq_len),
        columns[1].reshape(narrow * doc_count, seq_len),
    )
    mixing = mixing.astype(jnp.bfloat16).reshape(narrow, doc_count, seq_len)
    arrived = exchange_both(mixing, SEQ_CHAN, (SEQ, "chan"), (2, 2), (0, 0))
    row_mix = arrived.reshape(full_width, row_count).T
    summed = residual.reshape(row_count, full_width).astype(jnp.float32) + row_mix.astype(
        jnp.float32
    )
    normed = layer_norm(summed, gain_mix).astype(jnp.bfloat16)
    slot_count = max(2, 3 * row_count // n_seq)
    expert_ids = routing.reshape(-1)
    onehot = (expert_ids[:, None] == jnp.arange(n_seq, dtype=jnp.int32)[None, :]).astype(jnp.int32)
    before = jnp.cumsum(onehot, axis=0) - onehot
    slot_rank = jnp.sum(before * onehot, axis=1)
    target = (expert_ids * slot_count + slot_rank).reshape(quarter, doc_count).T.reshape(-1)
    placer = (jnp.arange(n_seq * slot_count, dtype=jnp.int32)[:, None] == target[None, :]).astype(
        jnp.bfloat16
    )
    outgoing = jnp.dot(placer, normed, preferred_element_type=jnp.float32).astype(jnp.bfloat16)
    outgoing = outgoing.reshape(n_seq, slot_count, full_width)
    weight_in = expert_in[0]
    weight_out = expert_out[0]
    slots = lax.all_to_all(outgoing, SEQ, split_axis=0, concat_axis=0, tiled=True)
    sources, count, unused = slots.shape
    inputs = slots.reshape(sources * count, full_width)
    hidden = jax.nn.gelu(jnp.dot(inputs, weight_in, preferred_element_type=jnp.float32)).astype(
        jnp.bfloat16
    )
    result = jnp.dot(hidden, weight_out, preferred_element_type=jnp.float32).astype(jnp.bfloat16)
    returned = lax.all_to_all(
        result.reshape(sources, count, full_width), SEQ, split_axis=0, concat_axis=0, tiled=True
    )
    combined = lax.dot_general(
        placer,
        returned.reshape(n_seq * slot_count, full_width),
        (((0,), (0,)), ((), ())),
        preferred_element_type=jnp.float32,
    )
    result = layer_norm(settle(normed).astype(jnp.float32) + combined, gain_out)
    return result.astype(jnp.bfloat16).reshape(doc_count, quarter, full_width)


def solution(mesh):
    torus = Mesh(
        mesh.devices.reshape(4, 4, 2, mesh.shape["chan"]), ("seq_0", "seq_1", "seq_2", "chan")
    )
    return jax.shard_map(
        local,
        mesh=torus,
        in_specs=(
            P(None, SEQ, "chan"),
            P(SEQ_CHAN, None),
            P(SEQ, None, None),
            P(SEQ, None, None),
            P(),
            P(),
        ),
        out_specs=P(None, SEQ_CHAN, None),
        check_vma=False,
    )
```

profile of v0, /device:TPU:1, one launch (start us, length us, event | category | flops | bytes accessed | tf_op | source)
XLA Modules:
  0.0 190.5 jit_solution(1428473528607769038)
XLA Ops:
  0.0 2.6 %broadcast_in_dim.2 = bf16[4,4,256,256]{3,2,1,0:T(8,128)(2,1)} broadcast(bf16[4,256,256]{2,1,0:T(8,128)(2,1)} %param.6), dimensions={1,2,3} | broadcast | bytes 2621440 | tf_op jit(solution)/shard_map/broadcast_in_dim | solution.py:20
  2.6 4.8 %all-to-all-start = ((bf16[4,4,256,256]{3,2,1,0:T(8,128)(2,1)}), bf16[4,4,256,256]{3,2,1,0:T(8,128)(2,1)S(1)}, u32[]{:S(2)}, u32[]{:S(2)}) async-start(bf16[4,4,256,256]{3,2,1,0:T(8,128)(2,1)} %broadcast_in_dim.2), calls=%async_computation | async-start | bytes 4194304 | tf_op jit(solution)/shard_map/all_to_all | solution.py:21
  7.4 4.9 %multiply_convert_fusion.3 = (bf16[256,1024]{1,0:T(8,128)(2,1)S(1)}, bf16[256,1024]{1,0:T(8,128)(2,1)S(1)}) fusion(s32[256]{0:T(256)S(1)} %iota_add_fusion), kind=kLoop, calls=%fused_computation.53 | loop fusion | flops 4980736 | bytes 1049600 | tf_op jit(solution)/shard_map/convert.5
  12.3 20.6 %all-to-all-done = bf16[4,4,256,256]{3,2,1,0:T(8,128)(2,1)S(1)} async-done(((bf16[4,4,256,256]{3,2,1,0:T(8,128)(2,1)}), bf16[4,4,256,256]{3,2,1,0:T(8,128)(2,1)S(1)}, u32[]{:S(2)}, u32[]{:S(2)}) %all-to-all-start) | async-done | bytes 2097184 | tf_op jit(solution)/shard_map/all_to_all | solution.py:21
  32.9 1.6 copy.65
  34.5 0.5 copy.85
  35.0 1.3 convolution_convert_fusion.1
  36.4 6.0 %all_to_all.30 = bf16[16,2,2,8,4,256]{5,3,4,0,2,1:T(8,128)(2,1)S(1)} all-to-all(bf16[16,2,2,8,4,256]{5,3,4,0,2,1:T(8,128)(2,1)S(1)} %copy.67), channel_id=1, replica_groups=mesh['seq_0'=4,'seq_1'=4,'seq_2'=2,'chan'=4] {'seq_2'}, dimensions={1} | all-to-all | bytes 2097152 | tf_op jit(solution)/shard_map/all_to_all | solution.py:38
  42.4 1.1 copy.68
  43.5 7.8 %all-to-all-start.2 = ((bf16[16,2,2,8,4,256]{5,3,4,1,2,0:T(8,128)(2,1)}), bf16[16,2,2,8,4,256]{5,3,4,1,2,0:T(8,128)(2,1)S(1)}, u32[]{:S(2)}, u32[]{:S(2)}) async-start(bf16[16,2,2,8,4,256]{5,3,4,1,2,0:T(8,128)(2,1)} %copy.68), calls=%async_computation.2 | async-start | bytes 2097152 | tf_op jit(solution)/shard_map/all_to_all | solution.py:38
  51.3 0.1 copy.77
  51.4 0.1 eq.53
  51.5 0.6 reduce-window.6
  52.1 0.1 fusion.87
  52.3 14.7 %all-to-all-done.2 = bf16[16,2,2,8,4,256]{5,3,4,1,2,0:T(8,128)(2,1)S(1)} async-done(((bf16[16,2,2,8,4,256]{5,3,4,1,2,0:T(8,128)(2,1)}), bf16[16,2,2,8,4,256]{5,3,4,1,2,0:T(8,128)(2,1)S(1)}, u32[]{:S(2)}, u32[]{:S(2)}) %all-to-all-start.2) | async-done | bytes 1048608 | tf_op jit(solution)/shard_map/all_to_all | solution.py:38
  67.0 0.9 fusion.148
  67.9 0.3 copy.70
  68.2 0.2 reshape_reshape_squeeze.6
  68.4 1.4 fusion.81
  69.8 1.4 fusion.83
  71.2 1.1 copy.71
  72.3 1.2 reshape_reshape_squeeze.7
  73.5 0.4 fusion.85
  73.9 0.4 fusion.79
  74.3 0.4 convolution_add_fusion.3
  74.7 0.4 copy-done.2
  75.2 0.4 convolution_add_fusion.5
  75.6 0.4 fusion.19
  76.0 0.4 fusion.21
  76.5 0.8 fusion.35
  77.3 0.8 fusion.23
  78.2 1.3 copy.72
  79.5 1.9 %convert_element_type.161 = bf16[8,4,32,256]{3,2,1,0:T(8,128)(2,1)S(1)} reshape(bf16[32,128,64]{2,1,0:T(8,128)(2,1)} %copy.72) | data formatting | bytes 1048576 | tf_op jit(solution)/shard_map/convert_element_type | solution.py:149
  81.4 0.3 fusion.149
  81.7 0.3 pad_maximum_fusion
  82.0 0.7 copy.73
  82.7 0.2 copy.88
  82.9 1.4 reshape.153
  84.3 6.7 %all-to-all-start.3 = ((bf16[128,2,1024]{2,1,0:T(2,128)(2,1)}), bf16[128,2,1024]{2,1,0:T(2,128)(2,1)S(1)}, u32[]{:S(2)}, u32[]{:S(2)}) async-start(bf16[128,2,1024]{2,1,0:T(2,128)(2,1)} %reshape.153), calls=%async_computation.3 | async-start | bytes 1048576 | tf_op jit(solution)/shard_map/all_to_all | solution.py:54
  91.0 0.2 slice_reduce_fusion
  91.1 0.1 eq.49
  91.4 0.1 reduce_sum.50
  91.7 2.4 %copy.63 = bf16[4,4,256,256]{2,3,0,1:T(8,128)(2,1)} copy(bf16[4,4,256,256]{3,2,1,0:T(8,128)(2,1)S(1)} %all-to-all-done) | data formatting | bytes 4194304 | tf_op jit(solution)/shard_map/all_to_all | solution.py:21
  94.0 1.6 constant_dynamic-slice_fusion
  95.6 0.3 copy.83
  96.0 9.1 %all-to-all-done.3 = bf16[128,2,1024]{2,1,0:T(2,128)(2,1)S(1)} async-done(((bf16[128,2,1024]{2,1,0:T(2,128)(2,1)}), bf16[128,2,1024]{2,1,0:T(2,128)(2,1)S(1)}, u32[]{:S(2)}, u32[]{:S(2)}) %all-to-all-start.3) | async-done | bytes 524320 | tf_op jit(solution)/shard_map/all_to_all | solution.py:54
  105.1 0.6 reshape.154
  105.7 0.3 convert_bitcast_fusion
  106.0 2.0 %copy.75 = f32[4,32,8,4,64]{4,3,2,1,0:T(4,128)} copy(f32[4,32,8,4,64]{4,2,3,0,1:T(8,128)S(1)} %convert_bitcast_fusion) | data formatting | bytes 2097152 | tf_op jit(solution)/shard_map/convert_element_type | solution.py:152
  107.9 2.5 %reshape.144 = f32[1024,256]{1,0:T(8,128)S(1)} reshape(f32[4,32,8,4,64]{4,3,2,1,0:T(4,128)} %copy.75) | data formatting | bytes 2097152 | tf_op jit(solution)/shard_map/convert_element_type | solution.py:152
  110.4 0.3 copy.76
  110.8 0.2 fusion.46
  111.0 0.3 multiply_reduce_fusion.1
  111.3 0.2 copy-done.5
  111.5 0.2 multiply_convert_fusion.1
  111.7 0.6 convolution_convert_fusion
  112.3 26.7 %all_to_all.31 = bf16[32,24,1024]{2,1,0:T(8,128)(2,1)} all-to-all(bf16[32,24,1024]{2,1,0:T(8,128)(2,1)S(1)} %bitcast.129), channel_id=1, replica_groups=mesh['seq_0'=4,'seq_1'=4,'seq_2'=2,'chan'=4] {'seq_0','seq_1','seq_2'}, dimensions={0} | all-to-all | bytes 3145728 | tf_op jit(solution)/shard_map/all_to_all | solution.py:169
  139.0 20.6 %fusion.14 = bf16[768,1024]{1,0:T(8,128)(2,1)} fusion(bf16[1,4096,1024]{2,1,0:T(8,128)(2,1)} %param.9, bf16[768,1024]{1,0:T(8,128)(2,1)} %bitcast.138, bf16[1,1024,4096]{2,1,0:T(8,128)(2,1)} %param.8), kind=kOutput, calls=%fused_computation.14 | convolution fusion | flops 12913999872 | bytes 19922944 | tf_op jit(solution)/shard_map/dot_general | solution.py:175
  159.6 3.8 %all-to-all-start.5 = ((bf16[32,24,1024]{2,1,0:T(8,128)(2,1)}), bf16[32,24,1024]{2,1,0:T(8,128)(2,1)S(1)}, u32[]{:S(2)}, u32[]{:S(2)}) async-start(bf16[32,24,1024]{2,1,0:T(8,128)(2,1)} %bitcast.137), calls=%async_computation.5 | async-start | bytes 3145728 | tf_op jit(solution)/shard_map/all_to_all | solution.py:176
  163.4 22.5 %all-to-all-done.5 = bf16[32,24,1024]{2,1,0:T(8,128)(2,1)S(1)} async-done(((bf16[32,24,1024]{2,1,0:T(8,128)(2,1)}), bf16[32,24,1024]{2,1,0:T(8,128)(2,1)S(1)}, u32[]{:S(2)}, u32[]{:S(2)}) %all-to-all-start.5) | async-done | bytes 1572896 | tf_op jit(solution)/shard_map/all_to_all | solution.py:176
  185.9 1.2 copy-done
  187.1 2.1 %fusion.150 = (f32[256]{0:T(256)S(1)}, f32[256,1024]{1,0:T(8,128)S(1)}) fusion(bf16[768,1024]{1,0:T(8,128)(2,1)} %bitcast.128, s32[256]{0:T(256)S(1)} %eq.57, bf16[256,1024]{1,0:T(8,128)(2,1)S(1)} %multiply_convert_fusion.1), kind=kOutput, calls=%fused_computation.179 | convolution fusion | flops 403635968 | bytes 3147776 | tf_op jit(solution)/shard_map/dot_general | solution.py:179
  189.2 0.3 multiply_reduce_fusion
  189.5 1.0 multiply_convert_fusion
  (25 shorter events, 0.6 us)
Async XLA Ops:
  2.6 30.3 %all-to-all-start = ((bf16[4,4,256,256]{3,2,1,0:T(8,128)(2,1)}), bf16[4,4,256,256]{3,2,1,0:T(8,128)(2,1)S(1)}, u32[]{:S(2)}, u32[]{:S(2)}) async-start(bf16[4,4,256,256]{3,2,1,0:T(8,128)(2,1)} %broadcast_in_dim.2), calls=%async_computation | async-start | bytes 4194304 | tf_op jit(solution)/shard_map/all_to_all | solution.py:21
  42.4 8.9 %copy-start.4 = (s32[64,4]{0,1:T(4,128)S(1)}, s32[64,4]{0,1:T(4,128)}, u32[]{:S(2)}) copy-start(s32[64,4]{0,1:T(4,128)} %param.7) | copy-start | bytes 3076
  43.5 23.4 %all-to-all-start.2 = ((bf16[16,2,2,8,4,256]{5,3,4,1,2,0:T(8,128)(2,1)}), bf16[16,2,2,8,4,256]{5,3,4,1,2,0:T(8,128)(2,1)S(1)}, u32[]{:S(2)}, u32[]{:S(2)}) async-start(bf16[16,2,2,8,4,256]{5,3,4,1,2,0:T(8,128)(2,1)} %copy.68), calls=%async_computation.2 | async-start | bytes 2097152 | tf_op jit(solution)/shard_map/all_to_all | solution.py:38
  68.4 2.8 %copy-start.3 = (bf16[1,8,4,32,256]{4,1,2,0,3:T(8,128)(2,1)S(1)}, bf16[1,8,4,32,256]{4,1,2,0,3:T(8,128)(2,1)}, u32[]{:S(2)}) copy-start(bf16[1,8,4,32,256]{4,1,2,0,3:T(8,128)(2,1)} %get-tuple-element.6) | copy-start | bytes 1572868
  73.9 1.2 copy-start.2
  74.3 1.3 copy-start.1
  84.3 20.8 %all-to-all-start.3 = ((bf16[128,2,1024]{2,1,0:T(2,128)(2,1)}), bf16[128,2,1024]{2,1,0:T(2,128)(2,1)S(1)}, u32[]{:S(2)}, u32[]{:S(2)}) async-start(bf16[128,2,1024]{2,1,0:T(2,128)(2,1)} %reshape.153), calls=%async_computation.3 | async-start | bytes 1048576 | tf_op jit(solution)/shard_map/all_to_all | solution.py:54
  110.8 0.7 copy-start.5
  159.6 26.3 %all-to-all-start.5 = ((bf16[32,24,1024]{2,1,0:T(8,128)(2,1)}), bf16[32,24,1024]{2,1,0:T(8,128)(2,1)S(1)}, u32[]{:S(2)}, u32[]{:S(2)}) async-start(bf16[32,24,1024]{2,1,0:T(8,128)(2,1)} %bitcast.137), calls=%async_computation.5 | async-start | bytes 3145728 | tf_op jit(solution)/shard_map/all_to_all | solution.py:176
  185.9 1.2 copy-start
  187.0 2.4 %copy-start.6 = (f32[1024]{0:T(1024)S(1)}, f32[1024]{0:T(1024)}, u32[]{:S(2)}) copy-start(f32[1024]{0:T(1024)} %param.11) | copy-start | bytes 12292
where the time goes:
time: 191 us; the launch traced here: 190 us
  waiting for transfers between devices  66.9 us (35%)
  blocking collectives  32.7 us (17%)
  matrix products  31.5 us (16%)
  local copies, waits for them, and re-layouts  27.7 us (15%)
  starting transfers between devices  23 us (12%)
  other arithmetic  8.29 us (4%)
    all_to_all x1, blocking collectives, local(): lax.all_to_all(outgoing, SEQ, split_axis=0, concat_axis=0, tiled=True)  26.7 us
    all_to_all x1, waiting for transfers between devices, local(): lax.all_to_all(result.reshape(sources, count, full_width), SEQ, split_axi...  22.5 us
    dot_general x1, matrix products, local(): jnp.dot(hidden, weight_out, preferred_element_type=jnp.float32)  20.6 us
    all_to_all x1, waiting for transfers between devices, sent_to_all(): return lax.all_to_all(copies, axis, split_axis=0, concat_axis=0, tiled=True)  20.6 us
    all_to_all x1, waiting for transfers between devices, exchange_in_order(): lax.all_to_all(parts, axes[k], split_axis=k, concat_axis=k, tiled=True)  14.7 us
    all_to_all x1, waiting for transfers between devices, exchange_both(): parts = lax.all_to_all(parts, axis, split_axis=0, concat_axis=0, tiled=True)  9.1 us
    all_to_all x1, starting transfers between devices, exchange_in_order(): lax.all_to_all(parts, axes[k], split_axis=k, concat_axis=k, tiled=True)  7.78 us
    all_to_all x1, starting transfers between devices, exchange_both(): parts = lax.all_to_all(parts, axis, split_axis=0, concat_axis=0, tiled=True)  6.68 us
  transfers between devices with their start and end apart: 4, of which 4 were waited for; matrix products, arithmetic and copies ran while one was open for 6% of the time, Pallas kernels for 0%

commit v1 on v0

v1 whole, which is shorter than its diff:
```python
import math

import jax
import jax.numpy as jnp
import numpy as np
from jax import lax
from jax.experimental import pallas as pl
from jax.experimental.pallas import tpu as pltpu
from jax.sharding import Mesh
from jax.sharding import PartitionSpec as P

SEQ = ("seq_0", "seq_1", "seq_2")
SEQ_CHAN = ("seq_0", "seq_1", "seq_2", "chan")

D = 1024
L = 8192
DOCS = 4
N_SEQ = 32
N_CHAN = 4
N_ALL = N_SEQ * N_CHAN
POS = L // N_SEQ
CH = D // N_CHAN
QUARTER = POS // N_CHAN
ROWS = DOCS * QUARTER
CH_OWN = CH // N_SEQ
SLOTS = 24
F32 = jnp.float32
BF16 = jnp.bfloat16
NN = (((1,), (0,)), ((), ()))
NT = (((1,), (1,)), ((), ()))
TN = (((0,), (0,)), ((), ()))


def mm(a, b, dims):
    return lax.dot_general(a, b, dims, preferred_element_type=F32)


def kernel_params(mib=48):
    return pltpu.CompilerParams(vmem_limit_bytes=mib << 20)


def twiddle_tables():
    k = np.arange(N_SEQ)[:, None]
    j = np.arange(POS)[None, :]
    angle = 2.0 * np.pi * ((k * j) % L) / L
    scale = 1.0 / math.sqrt(L)
    return (
        (np.cos(angle) * scale).astype(np.float32),
        (-np.sin(angle) * scale).astype(np.float32),
    )


def position_table():
    j = np.arange(POS)
    m = (np.arange(2)[:, None] + 2 * np.arange(POS // 2)[None, :]).reshape(-1)
    angle = 2.0 * np.pi * ((m[:, None] * j[None, :]) % POS) / POS
    cos, sin = np.cos(angle), np.sin(angle)
    return np.concatenate(
        [np.concatenate([cos, sin], 1), np.concatenate([sin, -cos], 1)], 0
    ).astype(BF16)


def hidden_tables():
    ch = np.arange(CH_OWN)[:, None, None]
    seq = np.arange(N_SEQ)[None, :, None]
    chan = np.arange(N_CHAN)[None, None, :]
    d = (chan * CH + seq * CH_OWN + ch).reshape(-1)
    f = np.arange(D // 2)
    angle = 2.0 * np.pi * ((d[:, None] * f[None, :]) % D) / D
    scale = 1.0 / math.sqrt(D)
    return (np.cos(angle) * scale).astype(BF16), (-np.sin(angle) * scale).astype(BF16)


def split_kernel(tok_ref, col_ref, row_ref):
    eye = (
        lax.broadcasted_iota(jnp.int32, (CH, CH), 0)
        == lax.broadcasted_iota(jnp.int32, (CH, CH), 1)
    ).astype(BF16)
    for pair in range(DOCS // 2):
        flipped = [
            mm(eye, tok_ref[2 * pair + i], NT).reshape(N_SEQ, CH_OWN, POS) for i in range(2)
        ]
        both = jnp.concatenate(flipped, axis=1).astype(BF16)
        col_ref[:, 2 * CH_OWN * pair : 2 * CH_OWN * (pair + 1), :] = both
    for q in range(N_CHAN):
        for doc in range(DOCS):
            row_ref[q, doc * QUARTER : (doc + 1) * QUARTER, :] = tok_ref[
                doc, q * QUARTER : (q + 1) * QUARTER, :
            ]


def split_tokens(tokens):
    return pl.pallas_call(
        split_kernel,
        out_shape=(
            jax.ShapeDtypeStruct((N_SEQ, DOCS * CH_OWN, POS), BF16),
            jax.ShapeDtypeStruct((N_CHAN, ROWS, CH), BF16),
        ),
        compiler_params=kernel_params(),
        name="split_tokens",
    )(tokens)


def real_fft(x):
    n = len(x)
    if n == 1:
        return [(x[0], None)]
    even = real_fft(x[0::2])
    odd = real_fft(x[1::2])
    if n == 2:
        return [(even[0][0] + odd[0][0], None), (even[0][0] - odd[0][0], None)]
    out = [None] * (n // 2 + 1)
    for k in range(n // 4 + 1):
        er, ei = even[k]
        orr, oi = odd[k]
        if k == 0:
            out[0] = (er + orr, None)
            out[n // 2] = (er - orr, None)
        elif 4 * k == n:
            out[k] = (er, -orr)
        else:
            c = math.cos(2.0 * math.pi * k / n)
            s = -math.sin(2.0 * math.pi * k / n)
            if 8 * k == n:
                tr, ti = (orr + oi) * c, (oi - orr) * c
            else:
                tr, ti = orr * c - oi * s, orr * s + oi * c
            out[k] = (er + tr, ei + ti)
            out[n // 2 - k] = (er - tr, ti - ei)
    return out


def sequence_kernel(x_ref, twr_ref, twi_ref, tab_ref, out_ref, t_ref, s_ref):
    for doc in range(DOCS):
        for half in range(POS // 128):
            lanes = slice(half * 128, (half + 1) * 128)
            lanes_im = slice(POS + half * 128, POS + (half + 1) * 128)
            rows = slice(doc * CH_OWN, (doc + 1) * CH_OWN)
            freq = real_fft([x_ref[s, rows, lanes].astype(F32) for s in range(N_SEQ)])
            for k in range(N_SEQ):
                if k <= N_SEQ // 2:
                    fr, fi = freq[k]
                else:
                    fr, fi = freq[N_SEQ - k]
                    fi = -fi
                wr = twr_ref[k : k + 1, lanes]
                wi = twi_ref[k : k + 1, lanes]
                if fi is None:
                    tr, ti = fr * wr, fr * wi
                else:
                    tr, ti = fr * wr - fi * wi, fr * wi + fi * wr
                t_ref[doc, k * CH_OWN : (k + 1) * CH_OWN, lanes] = tr
                t_ref[doc, k * CH_OWN : (k + 1) * CH_OWN, lanes_im] = ti
    for doc in range(DOCS):
        part = mm(tab_ref[...], t_ref[doc].astype(BF16), NT)
        for i in range(4):
            for h in range(2):
                s_ref[h, pl.ds(4 * i + doc, N_ALL, stride=16), :] = part[
                    i * N_ALL : (i + 1) * N_ALL, h * 128 : (h + 1) * 128
                ]
    for h in range(2):
        out_ref[:, :, h * 128 : (h + 1) * 128] = s_ref[h].reshape(N_ALL, 16, 128).astype(BF16)


def sequence_sums(cols):
    twr, twi = twiddle_tables()
    return pl.pallas_call(
        sequence_kernel,
        out_shape=jax.ShapeDtypeStruct((N_ALL, 16, N_SEQ * CH_OWN), BF16),
        scratch_shapes=[
            pltpu.VMEM((DOCS, N_SEQ * CH_OWN, 2 * POS), F32),
            pltpu.VMEM((2, N_ALL * 16, 128), F32),
        ],
        compiler_params=kernel_params(),
        name="sequence_sums",
    )(cols, jnp.asarray(twr), jnp.asarray(twi), jnp.asarray(position_table()))


def norm_rows(values, gain):
    center = values - jnp.mean(values, axis=-1, keepdims=True)
    spread = jnp.mean(center * center, axis=-1, keepdims=True)
    return center * lax.rsqrt(spread + 1e-05) * gain


def slot_map(ids):
    one = (lax.broadcasted_iota(jnp.int32, (N_SEQ, ROWS), 0) == ids).astype(F32)
    earlier = (
        lax.broadcasted_iota(jnp.int32, (ROWS, ROWS), 0)
        < lax.broadcasted_iota(jnp.int32, (ROWS, ROWS), 1)
    ).astype(BF16)
    before = mm(one.astype(BF16), earlier, NN)
    rank = jnp.sum(before * one, axis=0, keepdims=True).astype(jnp.int32)
    target = ids * SLOTS + rank
    slots = lax.broadcasted_iota(jnp.int32, (N_SEQ * SLOTS, ROWS), 0)
    return (slots == target).astype(BF16)


def mix_kernel(r_ref, res_ref, ids_ref, tc_ref, ts_ref, gain_ref, normed_ref, out_ref, s_ref, a_ref):
    lanes = N_SEQ * CH_OWN
    for h in range(2):
        s_ref[h] = r_ref[:, :, h * 128 : (h + 1) * 128].astype(F32).reshape(N_ALL * 16, 128)
    row = lax.broadcasted_iota(jnp.int32, (lanes, lanes), 0)
    col = lax.broadcasted_iota(jnp.int32, (lanes, lanes), 1)
    perm = ((row % N_SEQ == col // CH_OWN) & (row // N_SEQ == col % CH_OWN)).astype(BF16)
    for r in range(16):
        part, parity, doc = r // 8, (r // 4) % 2, r % 4
        block = jnp.concatenate(
            [s_ref[h, pl.ds(r, N_ALL, stride=16), :] for h in range(2)], axis=1
        ).astype(BF16)
        flipped = mm(perm, block, NT).astype(BF16)
        at = (doc * 2 + parity) * N_SEQ
        for ch in range(CH_OWN):
            base = part * D + ch * N_ALL
            a_ref[at : at + N_SEQ, base : base + N_ALL] = flipped[ch * N_SEQ : (ch + 1) * N_SEQ]
    cos_part = mm(a_ref[:, :D], tc_ref[...], NN)
    sin_part = mm(a_ref[:, D:], ts_ref[...], NN)
    half = D // 2
    sign = jnp.where(
        (lax.broadcasted_iota(jnp.int32, (D, 128), 0) // N_ALL) % 2 == 0, 1.0, -1.0
    ) * (1.0 / math.sqrt(D))
    middle = mm(a_ref[:, :D], sign.astype(BF16), NN)[:, :1]
    mirror = (
        lax.broadcasted_iota(jnp.int32, (half, half), 0)
        + lax.broadcasted_iota(jnp.int32, (half, half), 1)
        == half
    ).astype(BF16)
    low = (cos_part + sin_part).astype(BF16).astype(F32)
    high = mm((cos_part - sin_part).astype(BF16), mirror, NN)
    first = lax.broadcasted_iota(jnp.int32, (ROWS, half), 1) == 0
    high = jnp.where(first, middle.astype(BF16).astype(F32), high)
    mixing = jnp.concatenate([low, high], axis=1)
    residual = jnp.concatenate([res_ref[c].astype(F32) for c in range(N_CHAN)], axis=1)
    normed = norm_rows(residual + mixing, gain_ref[...]).astype(BF16)
    normed_ref[...] = normed
    out_ref[...] = mm(slot_map(ids_ref[...]), normed, NN).astype(BF16)


def mix_rows(parts, residual, ids, gain):
    tc, ts = hidden_tables()
    return pl.pallas_call(
        mix_kernel,
        out_shape=(
            jax.ShapeDtypeStruct((ROWS, D), BF16),
            jax.ShapeDtypeStruct((N_SEQ * SLOTS, D), BF16),
        ),
        scratch_shapes=[
            pltpu.VMEM((2, N_ALL * 16, 128), F32),
            pltpu.VMEM((ROWS, 2 * D), BF16),
        ],
        compiler_params=kernel_params(),
        name="mix_rows",
    )(parts, residual, ids, jnp.asarray(tc), jnp.asarray(ts), gain)


def finish_kernel(back_ref, normed_ref, ids_ref, gain_ref, out_ref):
    combined = mm(slot_map(ids_ref[...]), back_ref[...], TN)
    values = norm_rows(normed_ref[...].astype(F32) + combined, gain_ref[...])
    out_ref[...] = values.astype(BF16)


def finish_rows(back, normed, ids, gain):
    return pl.pallas_call(
        finish_kernel,
        out_shape=jax.ShapeDtypeStruct((ROWS, D), BF16),
        compiler_params=kernel_params(),
        name="finish_rows",
    )(back, normed, ids, gain)


def exchange(x, axes):
    return lax.all_to_all(x, axes, split_axis=0, concat_axis=0, tiled=True)


def local(tokens, routing, expert_in, expert_out, gain_mix, gain_out):
    ids = routing.T.reshape(1, ROWS)
    cols, rows = split_tokens(tokens)
    columns = exchange(cols, SEQ)
    residual = exchange(rows, "chan")
    parts = exchange(sequence_sums(columns), SEQ_CHAN)
    normed, outgoing = mix_rows(parts, residual, ids, gain_mix.reshape(1, D))
    slots = exchange(outgoing.reshape(N_SEQ, SLOTS, D), SEQ)
    inputs = slots.reshape(N_SEQ * SLOTS, D)
    hidden = jax.nn.gelu(mm(inputs, expert_in[0], NN)).astype(BF16)
    result = mm(hidden, expert_out[0], NN).astype(BF16)
    back = exchange(result.reshape(N_SEQ, SLOTS, D), SEQ)
    out = finish_rows(back.reshape(N_SEQ * SLOTS, D), normed, ids, gain_out.reshape(1, D))
    return out.reshape(DOCS, QUARTER, D)


def solution(mesh):
    torus = Mesh(
        mesh.devices.reshape(4, 4, 2, mesh.shape["chan"]), ("seq_0", "seq_1", "seq_2", "chan")
    )
    return jax.shard_map(
        local,
        mesh=torus,
        in_specs=(
            P(None, SEQ, "chan"),
            P(SEQ_CHAN, None),
            P(SEQ, None, None),
            P(SEQ, None, None),
            P(),
            P(),
        ),
        out_specs=P(None, SEQ_CHAN, None),
        check_vma=False,
    )
```

time: 191 us -> 143 us (0.75)
  waiting for transfers between devices: 66.9 us -> 23.5 us
  blocking collectives: 32.7 us -> 73.8 us
  local copies, waits for them, and re-layouts: 27.7 us -> 7.5 us
  starting transfers between devices: 23 us -> 8.29 us
  matrix products: 31.5 us -> 20.2 us
  Pallas kernels: 0 us -> 8.49 us
  other arithmetic: 8.29 us -> 0 us
    all_to_all x4 -> x2, waiting for transfers between devices: 66.9 us -> 23.5 us  [exchange(): return lax.all_to_all(x, axes, split_axis=0, concat_axis=0, tiled=True)]
    all_to_all x2 -> x3, blocking collectives: 32.7 us -> 73.8 us  [exchange(): return lax.all_to_all(x, axes, split_axis=0, concat_axis=0, tiled=True)]
    all_to_all x4 -> x2, starting transfers between devices: 23 us -> 8.29 us  [exchange(): return lax.all_to_all(x, axes, split_axis=0, concat_axis=0, tiled=True)]
    dot_general x14 -> x1, matrix products: 31.5 us -> 20.2 us  [mm(): return lax.dot_general(a, b, dims, preferred_element_type=F32)]
    pallas_call x0 -> x4, Pallas kernels: none -> 8.49 us  [the longest x1 2.93 us: mix_rows(): pl.pallas_call(mix_kernel, out_shape=(jax.ShapeDtypeStruct((ROWS, D), BF1...]
    convert_element_type x5 -> x0, local copies, waits for them, and re-layouts: 8.07 us -> none  [the longest x3 4.79 us: local(): row_mix.astype(jnp.float32)]
    another operation x3 -> x0, other arithmetic: 5.5 us -> none
    all_to_all x3 -> x0, local copies, waits for them, and re-layouts: 3.55 us -> none  [the longest x1 2.38 us: sent_to_all(): return lax.all_to_all(copies, axis, split_axis=0, concat_axis=0, tiled=True)]
  transfers between devices with their start and end apart: 4 -> 2, of which waited for: 4 -> 2; matrix products, arithmetic and copies ran while one was open for 6% -> 1% of each run, Pallas kernels for 0% -> 2%
where the time goes in v1:
time: 143 us; the launch traced here: 142 us
  blocking collectives  73.8 us (52%)
  waiting for transfers between devices  23.5 us (16%)
  matrix products  20.2 us (14%)
  Pallas kernels  8.49 us (6%)
  starting transfers between devices  8.29 us (6%)
  local copies, waits for them, and re-layouts  7.5 us (5%)
    all_to_all x3, blocking collectives, exchange(): return lax.all_to_all(x, axes, split_axis=0, concat_axis=0, tiled=True)  73.8 us
    all_to_all x2, waiting for transfers between devices, exchange(): return lax.all_to_all(x, axes, split_axis=0, concat_axis=0, tiled=True)  23.5 us
    dot_general x1, matrix products, mm(): return lax.dot_general(a, b, dims, preferred_element_type=F32)  20.2 us
    all_to_all x2, starting transfers between devices, exchange(): return lax.all_to_all(x, axes, split_axis=0, concat_axis=0, tiled=True)  8.29 us
    unnamed x16, local copies, waits for them, and re-layouts  6.74 us
    pallas_call x1, Pallas kernels, mix_rows(): pl.pallas_call(mix_kernel, out_shape=(jax.ShapeDtypeStruct((ROWS, D), BF1...  2.93 us
  transfers between devices with their start and end apart: 2, of which 2 were waited for; matrix products, arithmetic and copies ran while one was open for 1% of the time, Pallas kernels for 2%

profile of v1, /device:TPU:1, one launch (start us, length us, event | category | flops | bytes accessed | tf_op | source)
XLA Modules:
  0.0 141.8 jit_solution(12643036238911230852)
XLA Ops:
  0.0 0.0 copy-start.2
  0.0 1.0 copy-done.2
  1.0 1.1 split_tokens.1
  2.1 21.0 %all_to_all.25.x_ref = bf16[32,32,256]{2,1,0:T(8,128)(2,1)S(1)} all-to-all(bf16[32,32,256]{2,1,0:T(8,128)(2,1)S(1)} %get-tuple-element.9), channel_id=1, replica_groups=mesh['seq_0'=4,'seq_1'=4,'seq_2'=2,'chan'=4] {'seq_0','seq_1','seq_2'}, dimensions={0} | all-to-all | bytes 1048576 | tf_op jit(solution)/shard_map/all_to_all | solution.py:271
  23.1 4.0 %all-to-all-start.2 = ((bf16[4,256,256]{2,1,0:T(8,128)(2,1)}), bf16[4,256,256]{2,1,0:T(8,128)(2,1)S(1)}, u32[]{:S(2)}, u32[]{:S(2)}) async-start(bf16[4,256,256]{2,1,0:T(8,128)(2,1)} %get-tuple-element.10), calls=%async_computation.2 | async-start | bytes 1048576 | tf_op jit(solution)/shard_map/all_to_all | solution.py:271
  27.1 0.0 copy-start.3
  27.1 1.0 copy-done.3
  28.2 0.0 copy-start.4
  28.2 0.8 copy-done.4
  28.9 0.0 copy-start.5
  28.9 0.8 copy-done.5
  29.7 2.6 %sequence_sums.1 = bf16[128,16,256]{2,1,0:T(8,128)(2,1)} custom-call(bf16[32,32,256]{2,1,0:T(8,128)(2,1)S(1)} %all_to_all.25.x_ref, f32[32,256]{1,0:T(8,128)S(1)} %copy-done.5, f32[32,256]{1,0:T(8,128)S(1)} %copy-done.4, bf16[512,512]{1,0:T(8,128)(2,1)S(1)} %copy-done.3), custom_call_target="tpu_custom_call" | custom-call | tf_op jit(solution)/shard_map/sequence_sums/pallas_call | solution.py:167
  32.3 4.4 %all-to-all-done.2.res_ref = bf16[4,256,256]{2,1,0:T(8,128)(2,1)S(1)} async-done(((bf16[4,256,256]{2,1,0:T(8,128)(2,1)}), bf16[4,256,256]{2,1,0:T(8,128)(2,1)S(1)}, u32[]{:S(2)}, u32[]{:S(2)}) %all-to-all-start.2) | async-done | bytes 524320 | tf_op jit(solution)/shard_map/all_to_all | solution.py:271
  36.7 4.3 %all-to-all-start.1 = ((bf16[128,16,256]{2,1,0:T(8,128)(2,1)}), bf16[128,16,256]{2,1,0:T(8,128)(2,1)S(1)}, u32[]{:S(2)}, u32[]{:S(2)}) async-start(bf16[128,16,256]{2,1,0:T(8,128)(2,1)} %sequence_sums.1), calls=%async_computation.1 | async-start | bytes 2097152 | tf_op jit(solution)/shard_map/all_to_all | solution.py:271
  41.0 0.8 reshape.24.ids_ref
  41.7 19.1 %all-to-all-done.1.r_ref = bf16[128,16,256]{2,1,0:T(8,128)(2,1)S(1)} async-done(((bf16[128,16,256]{2,1,0:T(8,128)(2,1)}), bf16[128,16,256]{2,1,0:T(8,128)(2,1)S(1)}, u32[]{:S(2)}, u32[]{:S(2)}) %all-to-all-start.1) | async-done | bytes 1048608 | tf_op jit(solution)/shard_map/all_to_all | solution.py:271
  60.8 0.0 copy-start
  60.8 1.2 copy-done
  62.1 0.0 copy-start.1
  62.1 1.2 copy-done.1
  63.3 0.0 copy-start.6
  63.3 0.7 copy-done.6
  64.0 2.9 %mix_rows.1 = (bf16[256,1024]{1,0:T(8,128)(2,1)S(1)}, bf16[768,1024]{1,0:T(8,128)(2,1)S(1)}) custom-call(bf16[128,16,256]{2,1,0:T(8,128)(2,1)S(1)} %all-to-all-done.1.r_ref, bf16[4,256,256]{2,1,0:T(8,128)(2,1)S(1)} %all-to-all-done.2.res_ref, s32[1,256]{1,0:T(1,128)S(1)} %reshape.24.ids_ref, bf16[1024,512]{1,0:T(8,128)(2,1)S(1)} %copy-done.1, ...), custom_call_target="tpu_custom_call" | custom-call | tf_op jit(solution)/shard_map/mix_rows/pallas_call | solution.py:240
  66.9 26.4 %all_to_all.26 = bf16[32,24,1024]{2,1,0:T(8,128)(2,1)S(1)} all-to-all(bf16[32,24,1024]{2,1,0:T(8,128)(2,1)S(1)} %bitcast.22), channel_id=1, replica_groups=mesh['seq_0'=4,'seq_1'=4,'seq_2'=2,'chan'=4] {'seq_0','seq_1','seq_2'}, dimensions={0} | all-to-all | bytes 3145728 | tf_op jit(solution)/shard_map/all_to_all | solution.py:271
  93.3 0.0 copy-start.7
  93.3 20.2 %fusion.14 = bf16[768,1024]{1,0:T(8,128)(2,1)} fusion(bf16[1,4096,1024]{2,1,0:T(8,128)(2,1)} %param.14, bf16[768,1024]{1,0:T(8,128)(2,1)S(1)} %bitcast.25, bf16[1,1024,4096]{2,1,0:T(8,128)(2,1)} %param.13), kind=kOutput, calls=%fused_computation.13 | convolution fusion | flops 12913999872 | bytes 19922944 | tf_op jit(solution)/shard_map/dot_general | solution.py:35
  113.5 26.4 %all_to_all.27 = bf16[32,24,1024]{2,1,0:T(8,128)(2,1)S(1)} all-to-all(bf16[32,24,1024]{2,1,0:T(8,128)(2,1)} %bitcast.26), channel_id=1, replica_groups=mesh['seq_0'=4,'seq_1'=4,'seq_2'=2,'chan'=4] {'seq_0','seq_1','seq_2'}, dimensions={0} | all-to-all | bytes 3145728 | tf_op jit(solution)/shard_map/all_to_all | solution.py:271
  140.0 0.0 copy-done.7
  140.0 1.8 %finish_rows.1 = bf16[256,1024]{1,0:T(8,128)(2,1)} custom-call(bf16[768,1024]{1,0:T(8,128)(2,1)S(1)} %bitcast.21, bf16[256,1024]{1,0:T(8,128)(2,1)S(1)} %get-tuple-element.12.normed_ref, s32[1,256]{1,0:T(1,128)S(1)} %reshape.24.ids_ref, f32[1,1024]{1,0:T(1,128)S(1)} %bitcast.24), custom_call_target="tpu_custom_call" | custom-call | tf_op jit(solution)/shard_map/finish_rows/pallas_call | solution.py:262
Async XLA Ops:
  0.0 1.0 copy-start.2
  23.1 13.6 %all-to-all-start.2 = ((bf16[4,256,256]{2,1,0:T(8,128)(2,1)}), bf16[4,256,256]{2,1,0:T(8,128)(2,1)S(1)}, u32[]{:S(2)}, u32[]{:S(2)}) async-start(bf16[4,256,256]{2,1,0:T(8,128)(2,1)} %get-tuple-element.10), calls=%async_computation.2 | async-start | bytes 1048576 | tf_op jit(solution)/shard_map/all_to_all | solution.py:271
  27.1 1.0 copy-start.3
  28.2 0.8 copy-start.4
  28.9 0.8 copy-start.5
  36.7 24.2 %all-to-all-start.1 = ((bf16[128,16,256]{2,1,0:T(8,128)(2,1)}), bf16[128,16,256]{2,1,0:T(8,128)(2,1)S(1)}, u32[]{:S(2)}, u32[]{:S(2)}) async-start(bf16[128,16,256]{2,1,0:T(8,128)(2,1)} %sequence_sums.1), calls=%async_computation.1 | async-start | bytes 2097152 | tf_op jit(solution)/shard_map/all_to_all | solution.py:271
  60.8 1.2 copy-start
  62.1 1.2 copy-start.1
  63.3 0.7 copy-start.6
  93.3 46.7 %copy-start.7 = (f32[1024]{0:T(1024)S(1)}, f32[1024]{0:T(1024)}, u32[]{:S(2)}) copy-start(f32[1024]{0:T(1024)} %param.16) | copy-start | bytes 12292

commit v2 on v1

--- a/solution.py
+++ b/solution.py
@@ -23,7 +23,7 @@
 QUARTER = POS // N_CHAN
 ROWS = DOCS * QUARTER
 CH_OWN = CH // N_SEQ
-SLOTS = 24
+CHUNKS = ((0, 24),)
 F32 = jnp.float32
 BF16 = jnp.bfloat16
 NN = (((1,), (0,)), ((), ()))
@@ -35,7 +35,11 @@
     return lax.dot_general(a, b, dims, preferred_element_type=F32)
 
 
-def kernel_params(mib=48):
+def in_hbm(x):
+    return pltpu.with_memory_space_constraint(x, pltpu.HBM)
+
+
+def kernel_params(mib):
     return pltpu.CompilerParams(vmem_limit_bytes=mib << 20)
 
 
@@ -60,18 +64,41 @@
     ).astype(BF16)
 
 
+def tables_kernel(tc_ref, ts_ref):
+    block = 128
+    f = lax.broadcasted_iota(jnp.int32, (block, D // 2), 1)
+    for i in range(D // block):
+        row = lax.broadcasted_iota(jnp.int32, (block, D // 2), 0) + i * block
+        ch, owner = row // N_ALL, row % N_ALL
+        d = owner % N_CHAN * CH + owner // N_CHAN * CH_OWN + ch
+        turn = (d * f) % D
+        turn = jnp.where(turn >= D // 2, turn - D, turn)
+        angle = turn.astype(F32) * (2.0 * math.pi / D)
+        factor = 1.0 / math.sqrt(D)
+        rows = slice(i * block, (i + 1) * block)
+        tc_ref[rows, :] = (jnp.cos(angle) * factor).astype(BF16)
+        ts_ref[rows, :] = (-jnp.sin(angle) * factor).astype(BF16)
+
+
 def hidden_tables():
-    ch = np.arange(CH_OWN)[:, None, None]
-    seq = np.arange(N_SEQ)[None, :, None]
-    chan = np.arange(N_CHAN)[None, None, :]
-    d = (chan * CH + seq * CH_OWN + ch).reshape(-1)
-    f = np.arange(D // 2)
-    angle = 2.0 * np.pi * ((d[:, None] * f[None, :]) % D) / D
-    scale = 1.0 / math.sqrt(D)
-    return (np.cos(angle) * scale).astype(BF16), (-np.sin(angle) * scale).astype(BF16)
-
-
-def split_kernel(tok_ref, col_ref, row_ref):
+    return pl.pallas_call(
+        tables_kernel,
+        out_shape=(jax.ShapeDtypeStruct((D, D // 2), BF16),) * 2,
+        compiler_params=kernel_params(8),
+        name="hidden_tables",
+    )()
+
+
+def split_kernel(chan_ref, tok_ref, *refs):
+    n = (len(refs) - 2 - N_CHAN) // 2
+    tables, col_ref, row_refs = refs[:n], refs[n], refs[n + 1 : n + 1 + N_CHAN]
+    copies, sem = refs[n + 1 + N_CHAN : -1], refs[-1]
+    moves = [
+        pltpu.make_async_copy(src, dst, sem.at[i])
+        for i, (src, dst) in enumerate(zip(tables, copies))
+    ]
+    for move in moves:
+        move.start()
     eye = (
         lax.broadcasted_iota(jnp.int32, (CH, CH), 0)
         == lax.broadcasted_iota(jnp.int32, (CH, CH), 1)
@@ -82,23 +109,31 @@
         ]
         both = jnp.concatenate(flipped, axis=1).astype(BF16)
         col_ref[:, 2 * CH_OWN * pair : 2 * CH_OWN * (pair + 1), :] = both
-    for q in range(N_CHAN):
+    for i, row_ref in enumerate(row_refs):
+        first = pl.multiple_of((chan_ref[0] + i) % N_CHAN * QUARTER, QUARTER)
         for doc in range(DOCS):
-            row_ref[q, doc * QUARTER : (doc + 1) * QUARTER, :] = tok_ref[
-                doc, q * QUARTER : (q + 1) * QUARTER, :
+            row_ref[doc * QUARTER : (doc + 1) * QUARTER, :] = tok_ref[
+                doc, pl.ds(first, QUARTER), :
             ]
-
-
-def split_tokens(tokens):
-    return pl.pallas_call(
+    for move in moves:
+        move.wait()
+
+
+def split_tokens(chan_pos, tokens, *tables):
+    cols, *rest = pl.pallas_call(
         split_kernel,
         out_shape=(
             jax.ShapeDtypeStruct((N_SEQ, DOCS * CH_OWN, POS), BF16),
-            jax.ShapeDtypeStruct((N_CHAN, ROWS, CH), BF16),
+            *(jax.ShapeDtypeStruct((ROWS, CH), BF16) for _ in range(N_CHAN)),
+            *(jax.ShapeDtypeStruct(t.shape, t.dtype) for t in tables),
         ),
-        compiler_params=kernel_params(),
+        in_specs=[pl.BlockSpec(memory_space=pltpu.SMEM), pl.BlockSpec(memory_space=pltpu.VMEM)]
+        + [pl.BlockSpec(memory_space=pltpu.HBM)] * len(tables),
+        scratch_shapes=[pltpu.SemaphoreType.DMA((len(tables),))],
+        compiler_params=kernel_params(8),
         name="split_tokens",
-    )(tokens)
+    )(chan_pos, tokens, *map(in_hbm, tables))
+    return cols, rest[:N_CHAN], rest[N_CHAN:]
 
 
 def real_fft(x):
@@ -162,8 +197,7 @@
         out_ref[:, :, h * 128 : (h + 1) * 128] = s_ref[h].reshape(N_ALL, 16, 128).astype(BF16)
 
 
-def sequence_sums(cols):
-    twr, twi = twiddle_tables()
+def sequence_sums(cols, twr, twi, tab):
     return pl.pallas_call(
         sequence_kernel,
         out_shape=jax.ShapeDtypeStruct((N_ALL, 16, N_SEQ * CH_OWN), BF16),
@@ -171,9 +205,9 @@
             pltpu.VMEM((DOCS, N_SEQ * CH_OWN, 2 * POS), F32),
             pltpu.VMEM((2, N_ALL * 16, 128), F32),
         ],
-        compiler_params=kernel_params(),
+        compiler_params=kernel_params(24),
         name="sequence_sums",
-    )(cols, jnp.asarray(twr), jnp.asarray(twi), jnp.asarray(position_table()))
+    )(cols, twr, twi, tab)
 
 
 def norm_rows(values, gain):
@@ -182,7 +216,7 @@
     return center * lax.rsqrt(spread + 1e-05) * gain
 
 
-def slot_map(ids):
+def slot_maps(ids):
     one = (lax.broadcasted_iota(jnp.int32, (N_SEQ, ROWS), 0) == ids).astype(F32)
     earlier = (
         lax.broadcasted_iota(jnp.int32, (ROWS, ROWS), 0)
@@ -190,12 +224,20 @@
     ).astype(BF16)
     before = mm(one.astype(BF16), earlier, NN)
     rank = jnp.sum(before * one, axis=0, keepdims=True).astype(jnp.int32)
-    target = ids * SLOTS + rank
-    slots = lax.broadcasted_iota(jnp.int32, (N_SEQ * SLOTS, ROWS), 0)
-    return (slots == target).astype(BF16)
-
-
-def mix_kernel(r_ref, res_ref, ids_ref, tc_ref, ts_ref, gain_ref, normed_ref, out_ref, s_ref, a_ref):
+    maps = []
+    for start, count in CHUNKS:
+        inside = (rank >= start) & (rank < start + count)
+        target = jnp.where(inside, ids * count + rank - start, -1)
+        slots = lax.broadcasted_iota(jnp.int32, (N_SEQ * count, ROWS), 0)
+        maps.append((slots == target).astype(BF16))
+    return maps
+
+
+def mix_kernel(chan_ref, r_ref, *refs):
+    res_refs, (ids_ref, tc_ref, ts_ref, gain_ref, normed_ref) = refs[:N_CHAN], refs[N_CHAN : N_CHAN + 5]
+    *out_refs, s_ref, a_ref, x_ref = refs[N_CHAN + 5 :]
+    for i, res_ref in enumerate(res_refs):
+        x_ref[(chan_ref[0] + N_CHAN - i) % N_CHAN] = res_ref[...]
     lanes = N_SEQ * CH_OWN
     for h in range(2):
         s_ref[h] = r_ref[:, :, h * 128 : (h + 1) * 128].astype(F32).reshape(N_ALL * 16, 128)
@@ -229,42 +271,99 @@
     first = lax.broadcasted_iota(jnp.int32, (ROWS, half), 1) == 0
     high = jnp.where(first, middle.astype(BF16).astype(F32), high)
     mixing = jnp.concatenate([low, high], axis=1)
-    residual = jnp.concatenate([res_ref[c].astype(F32) for c in range(N_CHAN)], axis=1)
+    residual = jnp.concatenate([x_ref[c].astype(F32) for c in range(N_CHAN)], axis=1)
     normed = norm_rows(residual + mixing, gain_ref[...]).astype(BF16)
     normed_ref[...] = normed
-    out_ref[...] = mm(slot_map(ids_ref[...]), normed, NN).astype(BF16)
-
-
-def mix_rows(parts, residual, ids, gain):
-    tc, ts = hidden_tables()
+    for out_ref, chunk in zip(out_refs, slot_maps(ids_ref[...])):
+        out_ref[...] = mm(chunk, normed, NN).astype(BF16)
+
+
+def mix_rows(chan_pos, parts, residual, ids, tc, ts, gain):
     return pl.pallas_call(
         mix_kernel,
         out_shape=(
             jax.ShapeDtypeStruct((ROWS, D), BF16),
-            jax.ShapeDtypeStruct((N_SEQ * SLOTS, D), BF16),
+            *(jax.ShapeDtypeStruct((N_SEQ * count, D), BF16) for _, count in CHUNKS),
         ),
         scratch_shapes=[
             pltpu.VMEM((2, N_ALL * 16, 128), F32),
             pltpu.VMEM((ROWS, 2 * D), BF16),
+            pltpu.VMEM((N_CHAN, ROWS, CH), BF16),
         ],
-        compiler_params=kernel_params(),
+        in_specs=[pl.BlockSpec(memory_space=pltpu.SMEM)]
+        + [pl.BlockSpec(memory_space=pltpu.VMEM)] * (5 + N_CHAN),
+        compiler_params=kernel_params(24),
         name="mix_rows",
-    )(parts, residual, ids, jnp.asarray(tc), jnp.asarray(ts), gain)
-
-
-def finish_kernel(back_ref, normed_ref, ids_ref, gain_ref, out_ref):
-    combined = mm(slot_map(ids_ref[...]), back_ref[...], TN)
-    values = norm_rows(normed_ref[...].astype(F32) + combined, gain_ref[...])
-    out_ref[...] = values.astype(BF16)
+    )(chan_pos, parts, *residual, ids, tc, ts, gain)
+
+
+def gelu(v):
+    inner = math.sqrt(2.0 / math.pi)
+    return (0.5 * v) * (1.0 + jnp.tanh(v * (inner + (inner * 0.044715) * (v * v))))
+
+
+def expert_kernel(x_ref, wi_hbm, wo_hbm, out_ref, wi_ref, wo_ref, h_ref, sem):
+    ff = wi_ref.shape[1]
+    pieces, block, width = 8, 1024, 256
+    step = ff // pieces
+    moves = [
+        pltpu.make_async_copy(
+            wi_hbm.at[0, :, i * step : (i + 1) * step], wi_ref.at[:, i * step : (i + 1) * step], sem.at[i]
+        )
+        for i in range(pieces)
+    ] + [
+        pltpu.make_async_copy(
+            wo_hbm.at[0, i * step : (i + 1) * step], wo_ref.at[i * step : (i + 1) * step], sem.at[pieces + i]
+        )
+        for i in range(pieces)
+    ]
+    for move in moves:
+        move.start()
+    for i in range(ff // block):
+        for j in range(i * block // step, (i + 1) * block // step):
+            moves[j].wait()
+        cols = slice(i * block, (i + 1) * block)
+        h_ref[:, cols] = gelu(mm(x_ref[...], wi_ref[:, cols], NN)).astype(BF16)
+    for move in moves[pieces:]:
+        move.wait()
+    for n in range(D // width):
+        cols = slice(n * width, (n + 1) * width)
+        out_ref[:, cols] = mm(h_ref[...], wo_ref[:, cols], NN).astype(BF16)
+
+
+def expert_rows(x, expert_in, expert_out):
+    rows, ff = x.shape[0], expert_in.shape[2]
+    return pl.pallas_call(
+        expert_kernel,
+        out_shape=jax.ShapeDtypeStruct((rows, D), BF16),
+        in_specs=[pl.BlockSpec(memory_space=pltpu.VMEM)]
+        + [pl.BlockSpec(memory_space=pltpu.HBM)] * 2,
+        scratch_shapes=[
+            pltpu.VMEM((D, ff), BF16),
+            pltpu.VMEM((ff, D), BF16),
+            pltpu.VMEM((rows, ff), BF16),
+            pltpu.SemaphoreType.DMA((16,)),
+        ],
+        compiler_params=kernel_params(40),
+        name="expert_rows",
+    )(x, in_hbm(expert_in), in_hbm(expert_out))
+
+
+def finish_kernel(*refs):
+    *back_refs, normed_ref, ids_ref, gain_ref, out_ref = refs
+    values = normed_ref[...].astype(F32)
+    for back_ref, chunk in zip(back_refs, slot_maps(ids_ref[...])):
+        values = values + mm(chunk, back_ref[...], TN)
+    out_ref[...] = norm_rows(values, gain_ref[...]).astype(BF16)
 
 
 def finish_rows(back, normed, ids, gain):
     return pl.pallas_call(
         finish_kernel,
         out_shape=jax.ShapeDtypeStruct((ROWS, D), BF16),
-        compiler_params=kernel_params(),
+        compiler_params=kernel_params(24),
         name="finish_rows",
-    )(back, normed, ids, gain)
+    )(*back, normed, ids, gain)
 
 
 def exchange(x, axes):
@@ -273,18 +372,26 @@
 
 def local(tokens, routing, expert_in, expert_out, gain_mix, gain_out):
     ids = routing.T.reshape(1, ROWS)
-    cols, rows = split_tokens(tokens)
-    columns = exchange(cols, SEQ)
-    residual = exchange(rows, "chan")
-    parts = exchange(sequence_sums(columns), SEQ_CHAN)
-    normed, outgoing = mix_rows(parts, residual, ids, gain_mix.reshape(1, D))
-    slots = exchange(outgoing.reshape(N_SEQ, SLOTS, D), SEQ)
-    inputs = slots.reshape(N_SEQ * SLOTS, D)
-    hidden = jax.nn.gelu(mm(inputs, expert_in[0], NN)).astype(BF16)
-    result = mm(hidden, expert_out[0], NN).astype(BF16)
-    back = exchange(result.reshape(N_SEQ, SLOTS, D), SEQ)
-    out = finish_rows(back.reshape(N_SEQ * SLOTS, D), normed, ids, gain_out.reshape(1, D))
-    return out.reshape(DOCS, QUARTER, D)
+    chan_pos = lax.axis_index("chan").reshape(1)
+    tables = [*twiddle_tables(), position_table()]
+    cols, rows, tables = split_tokens(
+        chan_pos, tokens, *map(jnp.asarray, tables), gain_mix.reshape(1, D), gain_out.reshape(1, D)
+    )
+    twr, twi, tab, gain_mix, gain_out = tables
+    tc, ts = hidden_tables()
+    sums = sequence_sums(exchange(cols, SEQ), twr, twi, tab)
+    parts = exchange(sums, SEQ_CHAN)
+    residual = [rows[0]]
+    for i in range(1, N_CHAN):
+        ring = [(c, (c + i) % N_CHAN) for c in range(N_CHAN)]
+        residual.append(lax.ppermute(rows[i], "chan", ring))
+    normed, *outgoing = mix_rows(chan_pos, parts, residual, ids, tc, ts, gain_mix)
+    back = []
+    for (_, count), x in zip(CHUNKS, outgoing):
+        x = exchange(x.reshape(N_SEQ, count, D), SEQ).reshape(N_SEQ * count, D)
+        x = expert_rows(x, expert_in, expert_out)
+        back.append(exchange(x.reshape(N_SEQ, count, D), SEQ).reshape(N_SEQ * count, D))
+    return finish_rows(back, normed, ids, gain_out).reshape(DOCS, QUARTER, D)
 
 
 def solution(mesh):

time: 143 us -> 132 us (0.923)
  Pallas kernels: 8.49 us -> 36.8 us
  matrix products: 20.2 us -> 0 us
  waiting for transfers between devices: 23.5 us -> 6.01 us
  local copies, waits for them, and re-layouts: 7.5 us -> 1.13 us
  blocking collectives: 73.8 us -> 77.6 us
  starting transfers between devices: 8.29 us -> 10.5 us
    pallas_call x0 -> x2, Pallas kernels: none -> 26.3 us  [the longest x1 17.1 us: expert_rows(): pl.pallas_call(expert_kernel, out_shape=jax.ShapeDtypeStruct((rows, D), B...]
    all_to_all x2 -> x1, waiting for transfers between devices: 23.5 us -> 0.58 us  [exchange(): return lax.all_to_all(x, axes, split_axis=0, concat_axis=0, tiled=True)]
    dot_general x1 -> x0, matrix products: 20.2 us -> none  [mm(): return lax.dot_general(a, b, dims, preferred_element_type=F32)]
    unnamed x16 -> x4, local copies, waits for them, and re-layouts: 6.74 us -> 1.04 us
    ppermute x0 -> x3, waiting for transfers between devices: none -> 5.43 us  [local(): residual.append(lax.ppermute(rows[i], 'chan', ring))]
    ppermute x0 -> x3, starting transfers between devices: none -> 5 us  [local(): residual.append(lax.ppermute(rows[i], 'chan', ring))]
    all_to_all x3, blocking collectives: 73.8 us -> 77.6 us  [exchange(): return lax.all_to_all(x, axes, split_axis=0, concat_axis=0, tiled=True)]
    all_to_all x2 -> x1, starting transfers between devices: 8.29 us -> 5.51 us  [exchange(): return lax.all_to_all(x, axes, split_axis=0, concat_axis=0, tiled=True)]
  transfers between devices with their start and end apart: 2 -> 4, of which waited for: 2 -> 3; matrix products, arithmetic and copies ran while one was open for 1% -> 0% of each run, Pallas kernels for 2% -> 7%
where the time goes in v2:
time: 132 us
  blocking collectives  77.6 us (59%)
  Pallas kernels  36.8 us (28%)
  starting transfers between devices  10.5 us (8%)
  waiting for transfers between devices  6.01 us (5%)
    all_to_all x3, blocking collectives, exchange(): return lax.all_to_all(x, axes, split_axis=0, concat_axis=0, tiled=True)  77.6 us
    pallas_call x1, Pallas kernels, expert_rows(): pl.pallas_call(expert_kernel, out_shape=jax.ShapeDtypeStruct((rows, D), B...  17.1 us
    pallas_call x1, Pallas kernels, hidden_tables(): pl.pallas_call(tables_kernel, out_shape=(jax.ShapeDtypeStruct((D, D // 2)...  9.19 us
    all_to_all x1, starting transfers between devices, exchange(): return lax.all_to_all(x, axes, split_axis=0, concat_axis=0, tiled=True)  5.51 us
    ppermute x3, waiting for transfers between devices, local(): residual.append(lax.ppermute(rows[i], 'chan', ring))  5.43 us
    ppermute x3, starting transfers between devices, local(): residual.append(lax.ppermute(rows[i], 'chan', ring))  5 us
    pallas_call x1, Pallas kernels, mix_rows(): pl.pallas_call(mix_kernel, out_shape=(jax.ShapeDtypeStruct((ROWS, D), BF1...  4.04 us
    pallas_call x1, Pallas kernels, sequence_sums(): pl.pallas_call(sequence_kernel, out_shape=jax.ShapeDtypeStruct((N_ALL, 16...  2.64 us
  transfers between devices with their start and end apart: 4, of which 3 were waited for; matrix products, arithmetic and copies ran while one was open for 0% of the time, Pallas kernels for 7%

profile of v2, /device:TPU:1, one launch (start us, length us, event | category | flops | bytes accessed | tf_op | source)
XLA Modules:
  0.0 132.1 jit_solution(18273937872072108031)
XLA Ops:
  0.0 0.0 copy-start
  0.0 1.0 copy-done
  1.0 1.9 %split_tokens.1 = (bf16[32,32,256]{2,1,0:T(8,128)(2,1)S(1)}, bf16[256,256]{1,0:T(8,128)(2,1)S(1)}, bf16[256,256]{1,0:T(8,128)(2,1)}, bf16[256,256]{1,0:T(8,128)(...) custom-call(s32[1]{0:T(128)} %bitcast.chan_ref, ...), custom_call_target="tpu_custom_call" | custom-call | tf_op jit(solution)/shard_map/split_tokens/pallas_call | solution.py:123
  3.0 21.0 %all_to_all.20.x_ref = bf16[32,32,256]{2,1,0:T(8,128)(2,1)S(1)} all-to-all(bf16[32,32,256]{2,1,0:T(8,128)(2,1)S(1)} %get-tuple-element.19), channel_id=1, replica_groups=mesh['seq_0'=4,'seq_1'=4,'seq_2'=2,'chan'=4] {'seq_0','seq_1','seq_2'}, dimensions={0} | all-to-all | bytes 1048576 | tf_op jit(solution)/shard_map/all_to_all | solution.py:370
  23.9 2.6 %sequence_sums.1 = bf16[128,16,256]{2,1,0:T(8,128)(2,1)} custom-call(bf16[32,32,256]{2,1,0:T(8,128)(2,1)S(1)} %all_to_all.20.x_ref, f32[32,256]{1,0:T(8,128)S(1)} %get-tuple-element.20.twr_ref, f32[32,256]{1,0:T(8,128)S(1)} %get-tuple-element.21.twi_ref, bf16[512,512]{1,0:T(8,128)(2,1)S(1)} %get-tuple-element.22.tab_ref), custom_call_target="tpu_custom_call" | custom-call | tf_op jit(solution)/shard_map/sequence_sums/pallas_call | solution.py:201
  26.6 0.0 copy-start.1
  26.6 5.5 %all-to-all-start.1 = ((bf16[128,16,256]{2,1,0:T(8,128)(2,1)}), bf16[128,16,256]{2,1,0:T(8,128)(2,1)S(1)}, u32[]{:S(2)}, u32[]{:S(2)}) async-start(bf16[128,16,256]{2,1,0:T(8,128)(2,1)} %sequence_sums.1), calls=%async_computation.1 | async-start | bytes 2097152 | tf_op jit(solution)/shard_map/all_to_all | solution.py:370
  32.1 1.4 %collective-permute-start = (bf16[256,256]{1,0:T(8,128)(2,1)}, bf16[256,256]{1,0:T(8,128)(2,1)S(1)}, u32[]{:S(2)}, u32[]{:S(2)}) collective-permute-start(bf16[256,256]{1,0:T(8,128)(2,1)} %get-tuple-element.24), channel_id=1, source_target_pairs={{0,1},{1,2},{2,3},{3,0},{4,5},{5,6},{6,7},{7,4},{8,9},{9,10},{10,1... | collective-permute-start | bytes 393224 | tf_op jit(solution)/shard_map/ppermute | solution.py:387
  33.5 2.4 %collective-permute-start.1 = (bf16[256,256]{1,0:T(8,128)(2,1)}, bf16[256,256]{1,0:T(8,128)(2,1)S(1)}, u32[]{:S(2)}, u32[]{:S(2)}) collective-permute-start(bf16[256,256]{1,0:T(8,128)(2,1)} %get-tuple-element.25), channel_id=1, source_target_pairs={{0,2},{1,3},{2,0},{3,1},{4,6},{5,7},{6,4},{7,5},{8,10},{9,11},{10,... | collective-permute-start | bytes 393224 | tf_op jit(solution)/shard_map/ppermute | solution.py:387
  35.9 1.2 collective-permute-start.2
  37.1 9.2 %hidden_tables.1 = (bf16[1024,512]{1,0:T(8,128)(2,1)S(1)}, bf16[1024,512]{1,0:T(8,128)(2,1)S(1)}) custom-call(), custom_call_target="tpu_custom_call" | custom-call | tf_op jit(solution)/shard_map/hidden_tables/pallas_call | solution.py:84
  46.3 0.0 copy-done.1
  46.3 0.1 reshape.30.refs_4_.refs_2_
  46.4 2.3 %collective-permute-done.refs_1_ = bf16[256,256]{1,0:T(8,128)(2,1)S(1)} collective-permute-done((bf16[256,256]{1,0:T(8,128)(2,1)}, bf16[256,256]{1,0:T(8,128)(2,1)S(1)}, u32[]{:S(2)}, u32[]{:S(2)}) %collective-permute-start) | collective-permute-done | bytes 131104 | tf_op jit(solution)/shard_map/ppermute | solution.py:387
  48.7 3.1 %collective-permute-done.1.refs_2_ = bf16[256,256]{1,0:T(8,128)(2,1)S(1)} collective-permute-done((bf16[256,256]{1,0:T(8,128)(2,1)}, bf16[256,256]{1,0:T(8,128)(2,1)S(1)}, u32[]{:S(2)}, u32[]{:S(2)}) %collective-permute-start.1) | collective-permute-done | bytes 131104 | tf_op jit(solution)/shard_map/ppermute | solution.py:387
  51.8 0.0 collective-permute-done.2.refs_3_
  51.8 0.6 all-to-all-done.1.r_ref
  52.4 4.0 %mix_rows.1 = (bf16[256,1024]{1,0:T(8,128)(2,1)S(1)}, bf16[768,1024]{1,0:T(8,128)(2,1)S(1)}) custom-call(s32[1]{0:T(128)} %bitcast.chan_ref, bf16[128,16,256]{2,1,0:T(8,128)(2,1)S(1)} %all-to-all-done.1.r_ref, bf16[256,256]{1,0:T(8,128)(2,1)S(1)} %get-tuple-element.23.refs_0_, bf16[256,256]{1,0:T(8,128)(2,1)S(1)} %collective-permute-done.refs_1_, ...), custom_call_target="tpu_custom_call" | custom-call | tf_op jit(solution)/shard_map/mix_rows/pallas_call | solution.py:282
  56.4 30.4 %all_to_all.21 = bf16[32,24,1024]{2,1,0:T(8,128)(2,1)S(1)} all-to-all(bf16[32,24,1024]{2,1,0:T(8,128)(2,1)S(1)} %bitcast.12), channel_id=1, replica_groups=mesh['seq_0'=4,'seq_1'=4,'seq_2'=2,'chan'=4] {'seq_0','seq_1','seq_2'}, dimensions={0} | all-to-all | bytes 3145728 | tf_op jit(solution)/shard_map/all_to_all | solution.py:370
  86.8 17.1 %expert_rows.1 = bf16[768,1024]{1,0:T(8,128)(2,1)S(1)} custom-call(bf16[768,1024]{1,0:T(8,128)(2,1)S(1)} %bitcast.10, bf16[1,1024,4096]{2,1,0:T(8,128)(2,1)} %wi_hbm.1, bf16[1,4096,1024]{2,1,0:T(8,128)(2,1)} %wo_hbm.1), custom_call_target="tpu_custom_call" | custom-call | tf_op jit(solution)/shard_map/expert_rows/pallas_call | solution.py:336
  104.0 26.3 %all_to_all.22 = bf16[32,24,1024]{2,1,0:T(8,128)(2,1)S(1)} all-to-all(bf16[32,24,1024]{2,1,0:T(8,128)(2,1)S(1)} %bitcast.11), channel_id=1, replica_groups=mesh['seq_0'=4,'seq_1'=4,'seq_2'=2,'chan'=4] {'seq_0','seq_1','seq_2'}, dimensions={0} | all-to-all | bytes 3145728 | tf_op jit(solution)/shard_map/all_to_all | solution.py:370
  130.3 1.8 %finish_rows.1 = bf16[256,1024]{1,0:T(8,128)(2,1)} custom-call(bf16[768,1024]{1,0:T(8,128)(2,1)S(1)} %bitcast.9, bf16[256,1024]{1,0:T(8,128)(2,1)S(1)} %get-tuple-element.31.refs_1_, s32[1,256]{1,0:T(1,128)S(1)} %reshape.30.refs_4_.refs_2_, f32[1,1024]{1,0:T(1,128)S(1)} %get-tuple-element.32.refs_3_), custom_call_target="tpu_custom_call" | custom-call | tf_op jit(solution)/shard_map/finish_rows/pallas_call | solution.py:361
Async XLA Ops:
  0.0 1.0 copy-start
  26.6 19.7 %copy-start.1 = (s32[64,4]{0,1:T(4,128)S(1)}, s32[64,4]{0,1:T(4,128)}, u32[]{:S(2)}) copy-start(s32[64,4]{0,1:T(4,128)} %param.10) | copy-start | bytes 3076
  26.6 25.8 %all-to-all-start.1 = ((bf16[128,16,256]{2,1,0:T(8,128)(2,1)}), bf16[128,16,256]{2,1,0:T(8,128)(2,1)S(1)}, u32[]{:S(2)}, u32[]{:S(2)}) async-start(bf16[128,16,256]{2,1,0:T(8,128)(2,1)} %sequence_sums.1), calls=%async_computation.1 | async-start | bytes 2097152 | tf_op jit(solution)/shard_map/all_to_all | solution.py:370
  32.1 16.6 %collective-permute-start = (bf16[256,256]{1,0:T(8,128)(2,1)}, bf16[256,256]{1,0:T(8,128)(2,1)S(1)}, u32[]{:S(2)}, u32[]{:S(2)}) collective-permute-start(bf16[256,256]{1,0:T(8,128)(2,1)} %get-tuple-element.24), channel_id=1, source_target_pairs={{0,1},{1,2},{2,3},{3,0},{4,5},{5,6},{6,7},{7,4},{8,9},{9,10},{10,1... | collective-permute-start | bytes 393224 | tf_op jit(solution)/shard_map/ppermute | solution.py:387
  33.5 18.3 %collective-permute-start.1 = (bf16[256,256]{1,0:T(8,128)(2,1)}, bf16[256,256]{1,0:T(8,128)(2,1)S(1)}, u32[]{:S(2)}, u32[]{:S(2)}) collective-permute-start(bf16[256,256]{1,0:T(8,128)(2,1)} %get-tuple-element.25), channel_id=1, source_target_pairs={{0,2},{1,3},{2,0},{3,1},{4,6},{5,7},{6,4},{7,5},{8,10},{9,11},{10,... | collective-permute-start | bytes 393224 | tf_op jit(solution)/shard_map/ppermute | solution.py:387
  35.9 15.9 %collective-permute-start.2 = (bf16[256,256]{1,0:T(8,128)(2,1)}, bf16[256,256]{1,0:T(8,128)(2,1)}, u32[]{:S(2)}, u32[]{:S(2)}) collective-permute-start(bf16[256,256]{1,0:T(8,128)(2,1)} %get-tuple-element.26), channel_id=1, source_target_pairs={{0,3},{1,0},{2,1},{3,2},{4,7},{5,4},{6,5},{7,6},{8,11},{9,8},{10,9... | collective-permute-start | bytes 393224 | tf_op jit(solution)/shard_map/ppermute | solution.py:387

commit v3 on v2

--- a/solution.py
+++ b/solution.py
@@ -89,13 +89,10 @@
     )()
 
 
-def split_kernel(chan_ref, tok_ref, *refs):
-    n = (len(refs) - 2 - N_CHAN) // 2
-    tables, col_ref, row_refs = refs[:n], refs[n], refs[n + 1 : n + 1 + N_CHAN]
-    copies, sem = refs[n + 1 + N_CHAN : -1], refs[-1]
+def split_kernel(chan_ref, tok_hbm, col_ref, *refs):
+    *row_refs, tok_ref, sem = refs
     moves = [
-        pltpu.make_async_copy(src, dst, sem.at[i])
-        for i, (src, dst) in enumerate(zip(tables, copies))
+        pltpu.make_async_copy(tok_hbm.at[doc], tok_ref.at[doc], sem.at[doc]) for doc in range(DOCS)
     ]
     for move in moves:
         move.start()
@@ -104,36 +101,59 @@
         == lax.broadcasted_iota(jnp.int32, (CH, CH), 1)
     ).astype(BF16)
     for pair in range(DOCS // 2):
-        flipped = [
-            mm(eye, tok_ref[2 * pair + i], NT).reshape(N_SEQ, CH_OWN, POS) for i in range(2)
-        ]
+        flipped = []
+        for doc in (2 * pair, 2 * pair + 1):
+            moves[doc].wait()
+            flipped.append(mm(eye, tok_ref[doc], NT).reshape(N_SEQ, CH_OWN, POS))
         both = jnp.concatenate(flipped, axis=1).astype(BF16)
         col_ref[:, 2 * CH_OWN * pair : 2 * CH_OWN * (pair + 1), :] = both
     for i, row_ref in enumerate(row_refs):
-        first = pl.multiple_of((chan_ref[0] + i) % N_CHAN * QUARTER, QUARTER)
+        first = pl.multiple_of((chan_ref[0] + i + 1) % N_CHAN * QUARTER, QUARTER)
         for doc in range(DOCS):
             row_ref[doc * QUARTER : (doc + 1) * QUARTER, :] = tok_ref[
                 doc, pl.ds(first, QUARTER), :
             ]
-    for move in moves:
-        move.wait()
-
-
-def split_tokens(chan_pos, tokens, *tables):
-    cols, *rest = pl.pallas_call(
+
+
+def split_tokens(chan_pos, tokens):
+    cols, *rows = pl.pallas_call(
         split_kernel,
         out_shape=(
             jax.ShapeDtypeStruct((N_SEQ, DOCS * CH_OWN, POS), BF16),
-            *(jax.ShapeDtypeStruct((ROWS, CH), BF16) for _ in range(N_CHAN)),
-            *(jax.ShapeDtypeStruct(t.shape, t.dtype) for t in tables),
+            *(jax.ShapeDtypeStruct((ROWS, CH), BF16) for _ in range(N_CHAN - 1)),
         ),
-        in_specs=[pl.BlockSpec(memory_space=pltpu.SMEM), pl.BlockSpec(memory_space=pltpu.VMEM)]
-        + [pl.BlockSpec(memory_space=pltpu.HBM)] * len(tables),
-        scratch_shapes=[pltpu.SemaphoreType.DMA((len(tables),))],
+        in_specs=[
+            pl.BlockSpec(memory_space=pltpu.SMEM),
+            pl.BlockSpec(memory_space=pltpu.HBM),
+        ],
+        scratch_shapes=[
+            pltpu.VMEM((DOCS, POS, CH), BF16),
+            pltpu.SemaphoreType.DMA((DOCS,)),
+        ],
         compiler_params=kernel_params(8),
         name="split_tokens",
-    )(chan_pos, tokens, *map(in_hbm, tables))
-    return cols, rest[:N_CHAN], rest[N_CHAN:]
+    )(chan_pos, in_hbm(tokens))
+    return cols, rows
+
+
+def bring_kernel(*refs):
+    n = (len(refs) - 1) // 2
+    moves = [pltpu.make_async_copy(refs[i], refs[n + i], refs[-1].at[i]) for i in range(n)]
+    for move in moves:
+        move.start()
+    for move in moves:
+        move.wait()
+
+
+def bring(*arrays):
+    return pl.pallas_call(
+        bring_kernel,
+        out_shape=tuple(jax.ShapeDtypeStruct(t.shape, t.dtype) for t in arrays),
+        in_specs=[pl.BlockSpec(memory_space=pltpu.HBM)] * len(arrays),
+        scratch_shapes=[pltpu.SemaphoreType.DMA((len(arrays),))],
+        compiler_params=kernel_params(4),
+        name="bring",
+    )(*map(in_hbm, arrays))
 
 
 def real_fft(x):
@@ -233,11 +253,24 @@
     return maps
 
 
-def mix_kernel(chan_ref, r_ref, *refs):
-    res_refs, (ids_ref, tc_ref, ts_ref, gain_ref, normed_ref) = refs[:N_CHAN], refs[N_CHAN : N_CHAN + 5]
-    *out_refs, s_ref, a_ref, x_ref = refs[N_CHAN + 5 :]
-    for i, res_ref in enumerate(res_refs):
-        x_ref[(chan_ref[0] + N_CHAN - i) % N_CHAN] = res_ref[...]
+def mix_kernel(chan_ref, r_ref, tok_hbm, *refs):
+    res_refs, rest = refs[: N_CHAN - 1], refs[N_CHAN - 1 :]
+    ids_ref, tc_ref, ts_ref, gain_ref, normed_ref, *out_refs, s_ref, a_ref, x_ref, sem = rest
+    chan = chan_ref[0]
+    first = pl.multiple_of(chan * QUARTER, QUARTER)
+    moves = [
+        pltpu.make_async_copy(
+            tok_hbm.at[doc, pl.ds(first, QUARTER), :],
+            x_ref.at[chan, pl.ds(doc * QUARTER, QUARTER), :],
+            sem.at[N_CHAN - 1 + doc],
+        )
+        for doc in range(DOCS)
+    ] + [
+        pltpu.make_async_copy(res_ref, x_ref.at[(chan + N_CHAN - 1 - i) % N_CHAN], sem.at[i])
+        for i, res_ref in enumerate(res_refs)
+    ]
+    for move in moves:
+        move.start()
     lanes = N_SEQ * CH_OWN
     for h in range(2):
         s_ref[h] = r_ref[:, :, h * 128 : (h + 1) * 128].astype(F32).reshape(N_ALL * 16, 128)
@@ -271,6 +304,8 @@
     first = lax.broadcasted_iota(jnp.int32, (ROWS, half), 1) == 0
     high = jnp.where(first, middle.astype(BF16).astype(F32), high)
     mixing = jnp.concatenate([low, high], axis=1)
+    for move in moves:
+        move.wait()
     residual = jnp.concatenate([x_ref[c].astype(F32) for c in range(N_CHAN)], axis=1)
     normed = norm_rows(residual + mixing, gain_ref[...]).astype(BF16)
     normed_ref[...] = normed
@@ -278,7 +313,7 @@
         out_ref[...] = mm(chunk, normed, NN).astype(BF16)
 
 
-def mix_rows(chan_pos, parts, residual, ids, tc, ts, gain):
+def mix_rows(chan_pos, parts, tokens, residual, ids, tc, ts, gain):
     return pl.pallas_call(
         mix_kernel,
         out_shape=(
@@ -289,12 +324,14 @@
             pltpu.VMEM((2, N_ALL * 16, 128), F32),
             pltpu.VMEM((ROWS, 2 * D), BF16),
             pltpu.VMEM((N_CHAN, ROWS, CH), BF16),
+            pltpu.SemaphoreType.DMA((N_CHAN - 1 + DOCS,)),
         ],
-        in_specs=[pl.BlockSpec(memory_space=pltpu.SMEM)]
-        + [pl.BlockSpec(memory_space=pltpu.VMEM)] * (5 + N_CHAN),
+        in_specs=[pl.BlockSpec(memory_space=pltpu.SMEM), pl.BlockSpec(memory_space=pltpu.VMEM)]
+        + [pl.BlockSpec(memory_space=pltpu.HBM)] * N_CHAN
+        + [pl.BlockSpec(memory_space=pltpu.VMEM)] * 4,
         compiler_params=kernel_params(24),
         name="mix_rows",
-    )(chan_pos, parts, *residual, ids, tc, ts, gain)
+    )(chan_pos, parts, *map(in_hbm, (tokens, *residual)), ids, tc, ts, gain)
 
 
 def gelu(v):
@@ -373,19 +410,19 @@
 def local(tokens, routing, expert_in, expert_out, gain_mix, gain_out):
     ids = routing.T.reshape(1, ROWS)
     chan_pos = lax.axis_index("chan").reshape(1)
-    tables = [*twiddle_tables(), position_table()]
-    cols, rows, tables = split_tokens(
-        chan_pos, tokens, *map(jnp.asarray, tables), gain_mix.reshape(1, D), gain_out.reshape(1, D)
+    cols, rows = split_tokens(chan_pos, tokens)
+    tables = [jnp.asarray(t) for t in (*twiddle_tables(), position_table())]
+    twr, twi, tab, gain_mix, gain_out = bring(
+        *tables, gain_mix.reshape(1, D), gain_out.reshape(1, D)
     )
-    twr, twi, tab, gain_mix, gain_out = tables
     tc, ts = hidden_tables()
     sums = sequence_sums(exchange(cols, SEQ), twr, twi, tab)
     parts = exchange(sums, SEQ_CHAN)
-    residual = [rows[0]]
+    residual = []
     for i in range(1, N_CHAN):
         ring = [(c, (c + i) % N_CHAN) for c in range(N_CHAN)]
-        residual.append(lax.ppermute(rows[i], "chan", ring))
-    normed, *outgoing = mix_rows(chan_pos, parts, residual, ids, tc, ts, gain_mix)
+        residual.append(lax.ppermute(rows[i - 1], "chan", ring))
+    normed, *outgoing = mix_rows(chan_pos, parts, tokens, residual, ids, tc, ts, gain_mix)
     back = []
     for (_, count), x in zip(CHUNKS, outgoing):
         x = exchange(x.reshape(N_SEQ, count, D), SEQ).reshape(N_SEQ * count, D)

time: 132 us -> 132 us (level)
  blocking collectives: 77.6 us -> 56.7 us
  waiting for transfers between devices: 6.01 us -> 16.5 us
  starting transfers between devices: 10.5 us -> 20.1 us
  Pallas kernels: 36.8 us -> 38.3 us
    all_to_all x3 -> x2, blocking collectives: 77.6 us -> 56.7 us  [exchange(): return lax.all_to_all(x, axes, split_axis=0, concat_axis=0, tiled=True)]
    all_to_all x1 -> x2, waiting for transfers between devices: 0.58 us -> 10.9 us  [exchange(): return lax.all_to_all(x, axes, split_axis=0, concat_axis=0, tiled=True)]
    all_to_all x1 -> x2, starting transfers between devices: 5.51 us -> 15.1 us  [exchange(): return lax.all_to_all(x, axes, split_axis=0, concat_axis=0, tiled=True)]
  transfers between devices with their start and end apart: 4 -> 5, of which waited for: 3 -> 4; matrix products, arithmetic and copies ran while one was open for 0% -> 0% of each run, Pallas kernels for 7% -> 8%
where the time goes in v3:
time: 132 us
  blocking collectives  56.7 us (43%)
  Pallas kernels  38.3 us (29%)
  starting transfers between devices  20.1 us (15%)
  waiting for transfers between devices  16.5 us (12%)
    all_to_all x2, blocking collectives, exchange(): return lax.all_to_all(x, axes, split_axis=0, concat_axis=0, tiled=True)  56.7 us
    pallas_call x1, Pallas kernels, expert_rows(): pl.pallas_call(expert_kernel, out_shape=jax.ShapeDtypeStruct((rows, D), B...  17.2 us
    all_to_all x2, starting transfers between devices, exchange(): return lax.all_to_all(x, axes, split_axis=0, concat_axis=0, tiled=True)  15.1 us
    all_to_all x2, waiting for transfers between devices, exchange(): return lax.all_to_all(x, axes, split_axis=0, concat_axis=0, tiled=True)  10.9 us
    pallas_call x1, Pallas kernels, hidden_tables(): pl.pallas_call(tables_kernel, out_shape=(jax.ShapeDtypeStruct((D, D // 2)...  9.19 us
    ppermute x3, waiting for transfers between devices, local(): residual.append(lax.ppermute(rows[i - 1], 'chan', ring))  5.54 us
    ppermute x3, starting transfers between devices, local(): residual.append(lax.ppermute(rows[i - 1], 'chan', ring))  5 us
    pallas_call x1, Pallas kernels, mix_rows(): pl.pallas_call(mix_kernel, out_shape=(jax.ShapeDtypeStruct((ROWS, D), BF1...  3.53 us
  transfers between devices with their start and end apart: 5, of which 4 were waited for; matrix products, arithmetic and copies ran while one was open for 0% of the time, Pallas kernels for 8%

profile of v3, /device:TPU:1, one launch (start us, length us, event | category | flops | bytes accessed | tf_op | source)
XLA Modules:
  0.0 131.7 jit_solution(8795629796551762245)
XLA Ops:
  0.0 2.8 %split_tokens.1 = (bf16[32,32,256]{2,1,0:T(8,128)(2,1)}, bf16[256,256]{1,0:T(8,128)(2,1)S(1)}, bf16[256,256]{1,0:T(8,128)(2,1)S(1)}, bf16[256,256]{1,0:T(8,128)(2,1)S(1)}) custom-call(s32[1]{0:T(128)} %bitcast.chan_ref, bf16[4,256,256]{2,1,0:T(8,128)(2,1)} %tok_hbm.3), custom_call_target="tpu_custom_call" | custom-call | tf_op jit(solution)/shard_map/split_tokens/pallas_call | solution.py:119
  2.8 9.6 %all-to-all-start = ((bf16[32,32,256]{2,1,0:T(8,128)(2,1)}), bf16[32,32,256]{2,1,0:T(8,128)(2,1)S(1)}, u32[]{:S(2)}, u32[]{:S(2)}) async-start(bf16[32,32,256]{2,1,0:T(8,128)(2,1)} %get-tuple-element.18), calls=%async_computation | async-start | bytes 1048576 | tf_op jit(solution)/shard_map/all_to_all | solution.py:407
  12.4 1.1 bring.1
  13.5 10.5 %all-to-all-done.x_ref = bf16[32,32,256]{2,1,0:T(8,128)(2,1)S(1)} async-done(((bf16[32,32,256]{2,1,0:T(8,128)(2,1)}), bf16[32,32,256]{2,1,0:T(8,128)(2,1)S(1)}, u32[]{:S(2)}, u32[]{:S(2)}) %all-to-all-start) | async-done | bytes 524320 | tf_op jit(solution)/shard_map/all_to_all | solution.py:407
  24.0 2.6 %sequence_sums.1 = bf16[128,16,256]{2,1,0:T(8,128)(2,1)} custom-call(bf16[32,32,256]{2,1,0:T(8,128)(2,1)S(1)} %all-to-all-done.x_ref, f32[32,256]{1,0:T(8,128)S(1)} %get-tuple-element.19.twr_ref, f32[32,256]{1,0:T(8,128)S(1)} %get-tuple-element.20.twi_ref, bf16[512,512]{1,0:T(8,128)(2,1)S(1)} %get-tuple-element.21.tab_ref), custom_call_target="tpu_custom_call" | custom-call | tf_op jit(solution)/shard_map/sequence_sums/pallas_call | solution.py:221
  26.6 0.0 copy-start
  26.6 5.5 %all-to-all-start.1 = ((bf16[128,16,256]{2,1,0:T(8,128)(2,1)}), bf16[128,16,256]{2,1,0:T(8,128)(2,1)S(1)}, u32[]{:S(2)}, u32[]{:S(2)}) async-start(bf16[128,16,256]{2,1,0:T(8,128)(2,1)} %sequence_sums.1), calls=%async_computation.1 | async-start | bytes 2097152 | tf_op jit(solution)/shard_map/all_to_all | solution.py:407
  32.1 1.4 %collective-permute-start = (bf16[256,256]{1,0:T(8,128)(2,1)S(1)}, bf16[256,256]{1,0:T(8,128)(2,1)}, u32[]{:S(2)}, u32[]{:S(2)}) collective-permute-start(bf16[256,256]{1,0:T(8,128)(2,1)S(1)} %get-tuple-element.22), channel_id=1, source_target_pairs={{0,1},{1,2},{2,3},{3,0},{4,5},{5,6},{6,7},{7,4},{8,9},{9,10},{10,1... | collective-permute-start | bytes 393224 | tf_op jit(solution)/shard_map/ppermute | solution.py:424
  33.6 2.4 %collective-permute-start.1 = (bf16[256,256]{1,0:T(8,128)(2,1)S(1)}, bf16[256,256]{1,0:T(8,128)(2,1)}, u32[]{:S(2)}, u32[]{:S(2)}) collective-permute-start(bf16[256,256]{1,0:T(8,128)(2,1)S(1)} %get-tuple-element.23), channel_id=1, source_target_pairs={{0,2},{1,3},{2,0},{3,1},{4,6},{5,7},{6,4},{7,5},{8,10},{9,11},{10,... | collective-permute-start | bytes 393224 | tf_op jit(solution)/shard_map/ppermute | solution.py:424
  36.0 1.2 collective-permute-start.2
  37.1 9.2 %hidden_tables.1 = (bf16[1024,512]{1,0:T(8,128)(2,1)S(1)}, bf16[1024,512]{1,0:T(8,128)(2,1)S(1)}) custom-call(), custom_call_target="tpu_custom_call" | custom-call | tf_op jit(solution)/shard_map/hidden_tables/pallas_call | solution.py:84
  46.3 0.0 copy-done
  46.3 0.1 reshape.30.refs_3_.refs_2_
  46.4 2.4 %collective-permute-done.refs_0_ = bf16[256,256]{1,0:T(8,128)(2,1)} collective-permute-done((bf16[256,256]{1,0:T(8,128)(2,1)S(1)}, bf16[256,256]{1,0:T(8,128)(2,1)}, u32[]{:S(2)}, u32[]{:S(2)}) %collective-permute-start) | collective-permute-done | bytes 131104 | tf_op jit(solution)/shard_map/ppermute | solution.py:424
  48.9 3.1 %collective-permute-done.1.refs_1_ = bf16[256,256]{1,0:T(8,128)(2,1)} collective-permute-done((bf16[256,256]{1,0:T(8,128)(2,1)S(1)}, bf16[256,256]{1,0:T(8,128)(2,1)}, u32[]{:S(2)}, u32[]{:S(2)}) %collective-permute-start.1) | collective-permute-done | bytes 131104 | tf_op jit(solution)/shard_map/ppermute | solution.py:424
  52.0 0.0 collective-permute-done.2.refs_2_
  52.0 0.5 all-to-all-done.1.r_ref
  52.4 3.5 %mix_rows.1 = (bf16[256,1024]{1,0:T(8,128)(2,1)S(1)}, bf16[768,1024]{1,0:T(8,128)(2,1)S(1)}) custom-call(s32[1]{0:T(128)} %bitcast.chan_ref, bf16[128,16,256]{2,1,0:T(8,128)(2,1)S(1)} %all-to-all-done.1.r_ref, bf16[4,256,256]{2,1,0:T(8,128)(2,1)} %tok_hbm.3, bf16[256,256]{1,0:T(8,128)(2,1)} %collective-permute-done.refs_0_, ...), custom_call_target="tpu_custom_call" | custom-call | tf_op jit(solution)/shard_map/mix_rows/pallas_call | solution.py:317
  56.0 30.5 %all_to_all.20 = bf16[32,24,1024]{2,1,0:T(8,128)(2,1)S(1)} all-to-all(bf16[32,24,1024]{2,1,0:T(8,128)(2,1)S(1)} %bitcast.12), channel_id=1, replica_groups=mesh['seq_0'=4,'seq_1'=4,'seq_2'=2,'chan'=4] {'seq_0','seq_1','seq_2'}, dimensions={0} | all-to-all | bytes 3145728 | tf_op jit(solution)/shard_map/all_to_all | solution.py:407
  86.5 17.2 %expert_rows.1 = bf16[768,1024]{1,0:T(8,128)(2,1)S(1)} custom-call(bf16[768,1024]{1,0:T(8,128)(2,1)S(1)} %bitcast.10, bf16[1,1024,4096]{2,1,0:T(8,128)(2,1)} %wi_hbm.1, bf16[1,4096,1024]{2,1,0:T(8,128)(2,1)} %wo_hbm.1), custom_call_target="tpu_custom_call" | custom-call | tf_op jit(solution)/shard_map/expert_rows/pallas_call | solution.py:373
  103.6 26.2 %all_to_all.21 = bf16[32,24,1024]{2,1,0:T(8,128)(2,1)S(1)} all-to-all(bf16[32,24,1024]{2,1,0:T(8,128)(2,1)S(1)} %bitcast.11), channel_id=1, replica_groups=mesh['seq_0'=4,'seq_1'=4,'seq_2'=2,'chan'=4] {'seq_0','seq_1','seq_2'}, dimensions={0} | all-to-all | bytes 3145728 | tf_op jit(solution)/shard_map/all_to_all | solution.py:407
  129.9 1.8 %finish_rows.1 = bf16[256,1024]{1,0:T(8,128)(2,1)} custom-call(bf16[768,1024]{1,0:T(8,128)(2,1)S(1)} %bitcast.9, bf16[256,1024]{1,0:T(8,128)(2,1)S(1)} %get-tuple-element.29.refs_1_, s32[1,256]{1,0:T(1,128)S(1)} %reshape.30.refs_3_.refs_2_, f32[1,1024]{1,0:T(1,128)S(1)} %get-tuple-element.30.refs_3_), custom_call_target="tpu_custom_call" | custom-call | tf_op jit(solution)/shard_map/finish_rows/pallas_call | solution.py:398
Async XLA Ops:
  2.8 21.2 %all-to-all-start = ((bf16[32,32,256]{2,1,0:T(8,128)(2,1)}), bf16[32,32,256]{2,1,0:T(8,128)(2,1)S(1)}, u32[]{:S(2)}, u32[]{:S(2)}) async-start(bf16[32,32,256]{2,1,0:T(8,128)(2,1)} %get-tuple-element.18), calls=%async_computation | async-start | bytes 1048576 | tf_op jit(solution)/shard_map/all_to_all | solution.py:407
  26.6 19.7 %copy-start = (s32[64,4]{0,1:T(4,128)S(1)}, s32[64,4]{0,1:T(4,128)}, u32[]{:S(2)}) copy-start(s32[64,4]{0,1:T(4,128)} %param.10) | copy-start | bytes 3076
  26.6 25.8 %all-to-all-start.1 = ((bf16[128,16,256]{2,1,0:T(8,128)(2,1)}), bf16[128,16,256]{2,1,0:T(8,128)(2,1)S(1)}, u32[]{:S(2)}, u32[]{:S(2)}) async-start(bf16[128,16,256]{2,1,0:T(8,128)(2,1)} %sequence_sums.1), calls=%async_computation.1 | async-start | bytes 2097152 | tf_op jit(solution)/shard_map/all_to_all | solution.py:407
  32.1 16.7 %collective-permute-start = (bf16[256,256]{1,0:T(8,128)(2,1)S(1)}, bf16[256,256]{1,0:T(8,128)(2,1)}, u32[]{:S(2)}, u32[]{:S(2)}) collective-permute-start(bf16[256,256]{1,0:T(8,128)(2,1)S(1)} %get-tuple-element.22), channel_id=1, source_target_pairs={{0,1},{1,2},{2,3},{3,0},{4,5},{5,6},{6,7},{7,4},{8,9},{9,10},{10,1... | collective-permute-start | bytes 393224 | tf_op jit(solution)/shard_map/ppermute | solution.py:424
  33.6 18.4 %collective-permute-start.1 = (bf16[256,256]{1,0:T(8,128)(2,1)S(1)}, bf16[256,256]{1,0:T(8,128)(2,1)}, u32[]{:S(2)}, u32[]{:S(2)}) collective-permute-start(bf16[256,256]{1,0:T(8,128)(2,1)S(1)} %get-tuple-element.23), channel_id=1, source_target_pairs={{0,2},{1,3},{2,0},{3,1},{4,6},{5,7},{6,4},{7,5},{8,10},{9,11},{10,... | collective-permute-start | bytes 393224 | tf_op jit(solution)/shard_map/ppermute | solution.py:424
  36.0 16.0 %collective-permute-start.2 = (bf16[256,256]{1,0:T(8,128)(2,1)S(1)}, bf16[256,256]{1,0:T(8,128)(2,1)}, u32[]{:S(2)}, u32[]{:S(2)}) collective-permute-start(bf16[256,256]{1,0:T(8,128)(2,1)S(1)} %get-tuple-element.24), channel_id=1, source_target_pairs={{0,3},{1,0},{2,1},{3,2},{4,7},{5,4},{6,5},{7,6},{8,11},{9,8},{10,9... | collective-permute-start | bytes 393224 | tf_op jit(solution)/shard_map/ppermute | solution.py:424

commit v4 on v3

--- a/solution.py
+++ b/solution.py
@@ -22,7 +22,9 @@
 CH = D // N_CHAN
 QUARTER = POS // N_CHAN
 ROWS = DOCS * QUARTER
-CH_OWN = CH // N_SEQ
+CH_OWN = CH // N_ALL
+LANES = N_SEQ * DOCS * CH_OWN
+PARTS = 8
 CHUNKS = ((0, 24),)
 F32 = jnp.float32
 BF16 = jnp.bfloat16
@@ -67,10 +69,9 @@
 def tables_kernel(tc_ref, ts_ref):
     block = 128
     f = lax.broadcasted_iota(jnp.int32, (block, D // 2), 1)
-    for i in range(D // block):
-        row = lax.broadcasted_iota(jnp.int32, (block, D // 2), 0) + i * block
-        ch, owner = row // N_ALL, row % N_ALL
-        d = owner % N_CHAN * CH + owner // N_CHAN * CH_OWN + ch
+    for i in range(D // 2 // block):
+        owner = lax.broadcasted_iota(jnp.int32, (block, D // 2), 0)
+        d = i // CH_OWN * CH + CH_OWN * owner + i % CH_OWN
         turn = (d * f) % D
         turn = jnp.where(turn >= D // 2, turn - D, turn)
         angle = turn.astype(F32) * (2.0 * math.pi / D)
@@ -83,30 +84,35 @@
 def hidden_tables():
     return pl.pallas_call(
         tables_kernel,
-        out_shape=(jax.ShapeDtypeStruct((D, D // 2), BF16),) * 2,
+        out_shape=(jax.ShapeDtypeStruct((D // 2, D // 2), BF16),) * 2,
         compiler_params=kernel_params(8),
         name="hidden_tables",
     )()
 
 
 def split_kernel(chan_ref, tok_hbm, col_ref, *refs):
-    *row_refs, tok_ref, sem = refs
+    *row_refs, tok_ref, s_ref, sem = refs
     moves = [
         pltpu.make_async_copy(tok_hbm.at[doc], tok_ref.at[doc], sem.at[doc]) for doc in range(DOCS)
     ]
     for move in moves:
         move.start()
-    eye = (
-        lax.broadcasted_iota(jnp.int32, (CH, CH), 0)
-        == lax.broadcasted_iota(jnp.int32, (CH, CH), 1)
-    ).astype(BF16)
-    for pair in range(DOCS // 2):
-        flipped = []
-        for doc in (2 * pair, 2 * pair + 1):
-            moves[doc].wait()
-            flipped.append(mm(eye, tok_ref[doc], NT).reshape(N_SEQ, CH_OWN, POS))
-        both = jnp.concatenate(flipped, axis=1).astype(BF16)
-        col_ref[:, 2 * CH_OWN * pair : 2 * CH_OWN * (pair + 1), :] = both
+    row = lax.broadcasted_iota(jnp.int32, (CH, CH), 0)
+    index = CH_OWN * (row % N_ALL) + row // N_ALL
+    index = jnp.where(chan_ref[0] < N_CHAN // 2, index, (CH - index) % CH)
+    pick = (lax.broadcasted_iota(jnp.int32, (CH, CH), 1) == index).astype(BF16)
+    for doc in range(DOCS):
+        moves[doc].wait()
+        flipped = mm(pick, tok_ref[doc], NT)
+        for j in range(CH_OWN):
+            for h in range(POS // 128):
+                s_ref[h, pl.ds(doc * CH_OWN + j, N_ALL, stride=PARTS), :] = flipped[
+                    j * N_ALL : (j + 1) * N_ALL, h * 128 : (h + 1) * 128
+                ]
+    for h in range(POS // 128):
+        col_ref[:, :, h * 128 : (h + 1) * 128] = (
+            s_ref[h].reshape(N_ALL, PARTS, 128).astype(BF16)
+        )
     for i, row_ref in enumerate(row_refs):
         first = pl.multiple_of((chan_ref[0] + i + 1) % N_CHAN * QUARTER, QUARTER)
         for doc in range(DOCS):
@@ -119,7 +125,7 @@
     cols, *rows = pl.pallas_call(
         split_kernel,
         out_shape=(
-            jax.ShapeDtypeStruct((N_SEQ, DOCS * CH_OWN, POS), BF16),
+            jax.ShapeDtypeStruct((N_ALL, PARTS, POS), BF16),
             *(jax.ShapeDtypeStruct((ROWS, CH), BF16) for _ in range(N_CHAN - 1)),
         ),
         in_specs=[
@@ -128,6 +134,7 @@
         ],
         scratch_shapes=[
             pltpu.VMEM((DOCS, POS, CH), BF16),
+            pltpu.VMEM((POS // 128, N_ALL * PARTS, 128), F32),
             pltpu.SemaphoreType.DMA((DOCS,)),
         ],
         compiler_params=kernel_params(8),
@@ -185,13 +192,28 @@
     return out
 
 
-def sequence_kernel(x_ref, twr_ref, twi_ref, tab_ref, out_ref, t_ref, s_ref):
-    for doc in range(DOCS):
+def sequence_kernel(owner_ref, x_ref, twr_ref, twi_ref, tab_ref, out_ref, t_ref, s_ref):
+    rows = DOCS * CH_OWN
+    own_mirror = (lax.broadcasted_iota(jnp.int32, (rows, 128), 0) % CH_OWN == 0) & (
+        owner_ref[0] == 0
+    )
+
+    def folded(g, s, lanes):
+        third = x_ref[N_CHAN * s + 2, :, lanes].astype(F32)
+        fourth = x_ref[N_CHAN * s + 3, :, lanes].astype(F32)
+        base = x_ref[N_CHAN * s + g // 2, :, lanes].astype(F32)
+        if g == 0:
+            return base + jnp.where(own_mirror, 0.0, fourth)
+        if g == 1:
+            return jnp.where(own_mirror, third, base - fourth)
+        other = jnp.where(own_mirror, fourth, third)
+        return base + other if g == 2 else base - other
+
+    for g in range(4):
         for half in range(POS // 128):
             lanes = slice(half * 128, (half + 1) * 128)
             lanes_im = slice(POS + half * 128, POS + (half + 1) * 128)
-            rows = slice(doc * CH_OWN, (doc + 1) * CH_OWN)
-            freq = real_fft([x_ref[s, rows, lanes].astype(F32) for s in range(N_SEQ)])
+            freq = real_fft([folded(g, s, lanes) for s in range(N_SEQ)])
             for k in range(N_SEQ):
                 if k <= N_SEQ // 2:
                     fr, fi = freq[k]
@@ -204,30 +226,37 @@
                     tr, ti = fr * wr, fr * wi
                 else:
                     tr, ti = fr * wr - fi * wi, fr * wi + fi * wr
-                t_ref[doc, k * CH_OWN : (k + 1) * CH_OWN, lanes] = tr
-                t_ref[doc, k * CH_OWN : (k + 1) * CH_OWN, lanes_im] = ti
-    for doc in range(DOCS):
-        part = mm(tab_ref[...], t_ref[doc].astype(BF16), NT)
-        for i in range(4):
-            for h in range(2):
-                s_ref[h, pl.ds(4 * i + doc, N_ALL, stride=16), :] = part[
-                    i * N_ALL : (i + 1) * N_ALL, h * 128 : (h + 1) * 128
+                if g == 1:
+                    tr, ti = jnp.where(own_mirror, ti, tr), jnp.where(own_mirror, -tr, ti)
+                t_ref[g, k * rows : (k + 1) * rows, lanes] = tr
+                t_ref[g, k * rows : (k + 1) * rows, lanes_im] = ti
+    for g in range(4):
+        kind = slice(g % 2 * POS, (g % 2 + 1) * POS)
+        part = mm(tab_ref[kind, :], t_ref[g].astype(BF16), NT)
+        for parity in range(2):
+            for h in range(LANES // 128):
+                s_ref[h, pl.ds(2 * g + parity, N_ALL, stride=PARTS), :] = part[
+                    parity * N_ALL : (parity + 1) * N_ALL, h * 128 : (h + 1) * 128
                 ]
-    for h in range(2):
-        out_ref[:, :, h * 128 : (h + 1) * 128] = s_ref[h].reshape(N_ALL, 16, 128).astype(BF16)
-
-
-def sequence_sums(cols, twr, twi, tab):
+    for h in range(LANES // 128):
+        out_ref[:, :, h * 128 : (h + 1) * 128] = (
+            s_ref[h].reshape(N_ALL, PARTS, 128).astype(BF16)
+        )
+
+
+def sequence_sums(owner, cols, twr, twi, tab):
     return pl.pallas_call(
         sequence_kernel,
-        out_shape=jax.ShapeDtypeStruct((N_ALL, 16, N_SEQ * CH_OWN), BF16),
+        out_shape=jax.ShapeDtypeStruct((N_ALL, PARTS, LANES), BF16),
+        in_specs=[pl.BlockSpec(memory_space=pltpu.SMEM)]
+        + [pl.BlockSpec(memory_space=pltpu.VMEM)] * 4,
         scratch_shapes=[
-            pltpu.VMEM((DOCS, N_SEQ * CH_OWN, 2 * POS), F32),
-            pltpu.VMEM((2, N_ALL * 16, 128), F32),
+            pltpu.VMEM((4, LANES, 2 * POS), F32),
+            pltpu.VMEM((LANES // 128, N_ALL * PARTS, 128), F32),
         ],
         compiler_params=kernel_params(24),
         name="sequence_sums",
-    )(cols, twr, twi, tab)
+    )(owner, cols, twr, twi, tab)
 
 
 def norm_rows(values, gain):
@@ -271,29 +300,33 @@
     ]
     for move in moves:
         move.start()
-    lanes = N_SEQ * CH_OWN
-    for h in range(2):
-        s_ref[h] = r_ref[:, :, h * 128 : (h + 1) * 128].astype(F32).reshape(N_ALL * 16, 128)
-    row = lax.broadcasted_iota(jnp.int32, (lanes, lanes), 0)
-    col = lax.broadcasted_iota(jnp.int32, (lanes, lanes), 1)
-    perm = ((row % N_SEQ == col // CH_OWN) & (row // N_SEQ == col % CH_OWN)).astype(BF16)
-    for r in range(16):
-        part, parity, doc = r // 8, (r // 4) % 2, r % 4
+    for h in range(LANES // 128):
+        s_ref[h] = r_ref[:, :, h * 128 : (h + 1) * 128].astype(F32).reshape(N_ALL * PARTS, 128)
+    row = lax.broadcasted_iota(jnp.int32, (LANES, LANES), 0)
+    at = row % N_SEQ * (DOCS * CH_OWN) + row // N_SEQ % DOCS * CH_OWN + row // (N_SEQ * DOCS)
+    perm = (lax.broadcasted_iota(jnp.int32, (LANES, LANES), 1) == at).astype(BF16)
+    half = D // 2
+    for r in range(PARTS):
+        g, parity = r // 2, r % 2
         block = jnp.concatenate(
-            [s_ref[h, pl.ds(r, N_ALL, stride=16), :] for h in range(2)], axis=1
+            [s_ref[h, pl.ds(r, N_ALL, stride=PARTS), :] for h in range(LANES // 128)], axis=1
         ).astype(BF16)
         flipped = mm(perm, block, NT).astype(BF16)
-        at = (doc * 2 + parity) * N_SEQ
-        for ch in range(CH_OWN):
-            base = part * D + ch * N_ALL
-            a_ref[at : at + N_SEQ, base : base + N_ALL] = flipped[ch * N_SEQ : (ch + 1) * N_SEQ]
-    cos_part = mm(a_ref[:, :D], tc_ref[...], NN)
-    sin_part = mm(a_ref[:, D:], ts_ref[...], NN)
-    half = D // 2
+        for j in range(CH_OWN):
+            base = g % 2 * half + g // 2 * CH + j * N_ALL
+            for doc in range(DOCS):
+                first = (doc * 2 + parity) * N_SEQ
+                start = (j * DOCS + doc) * N_SEQ
+                a_ref[first : first + N_SEQ, base : base + N_ALL] = flipped[start : start + N_SEQ]
+    factor = 1.0 / math.sqrt(D)
+    own = a_ref[:, half : half + 1].astype(F32) * factor
+    swing = 1.0 - 2.0 * (lax.broadcasted_iota(jnp.int32, (ROWS, half), 1) % 2).astype(F32)
+    cos_part = mm(a_ref[:, :half], tc_ref[...], NN) + own * swing
+    sin_part = mm(a_ref[:, half:], ts_ref[...], NN)
     sign = jnp.where(
-        (lax.broadcasted_iota(jnp.int32, (D, 128), 0) // N_ALL) % 2 == 0, 1.0, -1.0
-    ) * (1.0 / math.sqrt(D))
-    middle = mm(a_ref[:, :D], sign.astype(BF16), NN)[:, :1]
+        lax.broadcasted_iota(jnp.int32, (half, 128), 0) // N_ALL % CH_OWN == 0, factor, -factor
+    )
+    middle = mm(a_ref[:, :half], sign.astype(BF16), NN)[:, :1] + own
     mirror = (
         lax.broadcasted_iota(jnp.int32, (half, half), 0)
         + lax.broadcasted_iota(jnp.int32, (half, half), 1)
@@ -321,8 +354,8 @@
             *(jax.ShapeDtypeStruct((N_SEQ * count, D), BF16) for _, count in CHUNKS),
         ),
         scratch_shapes=[
-            pltpu.VMEM((2, N_ALL * 16, 128), F32),
-            pltpu.VMEM((ROWS, 2 * D), BF16),
+            pltpu.VMEM((LANES // 128, N_ALL * PARTS, 128), F32),
+            pltpu.VMEM((ROWS, D), BF16),
             pltpu.VMEM((N_CHAN, ROWS, CH), BF16),
             pltpu.SemaphoreType.DMA((N_CHAN - 1 + DOCS,)),
         ],
@@ -410,13 +443,14 @@
 def local(tokens, routing, expert_in, expert_out, gain_mix, gain_out):
     ids = routing.T.reshape(1, ROWS)
     chan_pos = lax.axis_index("chan").reshape(1)
+    owner = lax.axis_index(SEQ_CHAN).reshape(1)
     cols, rows = split_tokens(chan_pos, tokens)
     tables = [jnp.asarray(t) for t in (*twiddle_tables(), position_table())]
     twr, twi, tab, gain_mix, gain_out = bring(
         *tables, gain_mix.reshape(1, D), gain_out.reshape(1, D)
     )
     tc, ts = hidden_tables()
-    sums = sequence_sums(exchange(cols, SEQ), twr, twi, tab)
+    sums = sequence_sums(owner, exchange(cols, SEQ_CHAN), twr, twi, tab)
     parts = exchange(sums, SEQ_CHAN)
     residual = []
     for i in range(1, N_CHAN):

time: 132 us -> 128 us (0.970)
  Pallas kernels: 38.3 us -> 32 us
  waiting for transfers between devices: 16.5 us -> 18.1 us
    pallas_call x3, Pallas kernels: 14.6 us -> 9.18 us  [the longest x1 4.5 us: hidden_tables(): pl.pallas_call(tables_kernel, out_shape=(jax.ShapeDtypeStruct((D // 2, D...]
    all_to_all x2, waiting for transfers between devices: 10.9 us -> 13.6 us  [exchange(): return lax.all_to_all(x, axes, split_axis=0, concat_axis=0, tiled=True)]
  transfers between devices with their start and end apart: 5 -> 5, of which waited for: 4 -> 4; matrix products, arithmetic and copies ran while one was open for 0% -> 0% of each run, Pallas kernels for 8% -> 4%
where the time goes in v4:
time: 128 us
  blocking collectives  57.3 us (45%)
  Pallas kernels  32 us (25%)
  starting transfers between devices  20.1 us (16%)
  waiting for transfers between devices  18.1 us (14%)
    all_to_all x2, blocking collectives, exchange(): return lax.all_to_all(x, axes, split_axis=0, concat_axis=0, tiled=True)  57.3 us
    pallas_call x1, Pallas kernels, expert_rows(): pl.pallas_call(expert_kernel, out_shape=jax.ShapeDtypeStruct((rows, D), B...  17.2 us
    all_to_all x2, starting transfers between devices, exchange(): return lax.all_to_all(x, axes, split_axis=0, concat_axis=0, tiled=True)  15.1 us
    all_to_all x2, waiting for transfers between devices, exchange(): return lax.all_to_all(x, axes, split_axis=0, concat_axis=0, tiled=True)  13.6 us
    ppermute x3, starting transfers between devices, local(): residual.append(lax.ppermute(rows[i - 1], 'chan', ring))  5 us
    pallas_call x1, Pallas kernels, hidden_tables(): pl.pallas_call(tables_kernel, out_shape=(jax.ShapeDtypeStruct((D // 2, D...  4.5 us
    ppermute x3, waiting for transfers between devices, local(): residual.append(lax.ppermute(rows[i - 1], 'chan', ring))  4.5 us
    pallas_call x1, Pallas kernels, split_tokens(): pl.pallas_call(split_kernel, out_shape=(jax.ShapeDtypeStruct((N_ALL, PART...  2.8 us
  transfers between devices with their start and end apart: 5, of which 4 were waited for; matrix products, arithmetic and copies ran while one was open for 0% of the time, Pallas kernels for 4%

profile of v4, /device:TPU:1, one launch (start us, length us, event | category | flops | bytes accessed | tf_op | source)
XLA Modules:
  0.0 127.7 jit_solution(15811034468888736475)
XLA Ops:
  0.0 2.8 %split_tokens.1 = (bf16[128,8,256]{2,1,0:T(8,128)(2,1)}, bf16[256,256]{1,0:T(8,128)(2,1)S(1)}, bf16[256,256]{1,0:T(8,128)(2,1)S(1)}, bf16[256,256]{1,0:T(8,128)(2,1)S(1)}) custom-call(s32[1]{0:T(128)} %bitcast.chan_ref, bf16[4,256,256]{2,1,0:T(8,128)(2,1)} %tok_hbm.3), custom_call_target="tpu_custom_call" | custom-call | tf_op jit(solution)/shard_map/split_tokens/pallas_call | solution.py:125
  2.8 11.5 %all-to-all-start = ((bf16[128,8,256]{2,1,0:T(8,128)(2,1)}), bf16[128,8,256]{2,1,0:T(8,128)(2,1)S(1)}, u32[]{:S(2)}, u32[]{:S(2)}) async-start(bf16[128,8,256]{2,1,0:T(8,128)(2,1)} %get-tuple-element.18), calls=%async_computation | async-start | bytes 1048576 | tf_op jit(solution)/shard_map/all_to_all | solution.py:440
  14.3 0.0 copy-start.3
  14.3 1.1 bring.1
  15.5 12.9 %all-to-all-done.x_ref = bf16[128,8,256]{2,1,0:T(8,128)(2,1)S(1)} async-done(((bf16[128,8,256]{2,1,0:T(8,128)(2,1)}), bf16[128,8,256]{2,1,0:T(8,128)(2,1)S(1)}, u32[]{:S(2)}, u32[]{:S(2)}) %all-to-all-start) | async-done | bytes 524320 | tf_op jit(solution)/shard_map/all_to_all | solution.py:440
  28.4 1.9 %sequence_sums.1 = bf16[128,8,256]{2,1,0:T(8,128)(2,1)} custom-call(s32[1]{0:T(128)} %bitcast.1.owner_ref, bf16[128,8,256]{2,1,0:T(8,128)(2,1)S(1)} %all-to-all-done.x_ref, f32[32,256]{1,0:T(8,128)S(1)} %get-tuple-element.19.twr_ref, f32[32,256]{1,0:T(8,128)S(1)} %get-tuple-element.20.twi_ref, bf16[512,512]{1,0:T(8,128)(2,1)S(1)} %get-tuple-element.21.tab_ref), custom_call_target="tpu_custom_call" | custom-call | tf_op jit(solution)/shard_map/sequence_sums/pallas_call | solution.py:248
  30.3 3.6 %all-to-all-start.1 = ((bf16[128,8,256]{2,1,0:T(8,128)(2,1)}), bf16[128,8,256]{2,1,0:T(8,128)(2,1)S(1)}, u32[]{:S(2)}, u32[]{:S(2)}) async-start(bf16[128,8,256]{2,1,0:T(8,128)(2,1)} %sequence_sums.1), calls=%async_computation.1 | async-start | bytes 1048576 | tf_op jit(solution)/shard_map/all_to_all | solution.py:440
  33.9 1.4 %collective-permute-start = (bf16[256,256]{1,0:T(8,128)(2,1)S(1)}, bf16[256,256]{1,0:T(8,128)(2,1)S(1)}, u32[]{:S(2)}, u32[]{:S(2)}) collective-permute-start(bf16[256,256]{1,0:T(8,128)(2,1)S(1)} %get-tuple-element.22), channel_id=1, source_target_pairs={{0,1},{1,2},{2,3},{3,0},{4,5},{5,6},{6,7},{7,4},{8,9},{9,10},{10,1... | collective-permute-start | bytes 393224 | tf_op jit(solution)/shard_map/ppermute | solution.py:458
  35.3 2.4 %collective-permute-start.1 = (bf16[256,256]{1,0:T(8,128)(2,1)S(1)}, bf16[256,256]{1,0:T(8,128)(2,1)S(1)}, u32[]{:S(2)}, u32[]{:S(2)}) collective-permute-start(bf16[256,256]{1,0:T(8,128)(2,1)S(1)} %get-tuple-element.23), channel_id=1, source_target_pairs={{0,2},{1,3},{2,0},{3,1},{4,6},{5,7},{6,4},{7,5},{8,10},{9,11},{10,... | collective-permute-start | bytes 393224 | tf_op jit(solution)/shard_map/ppermute | solution.py:458
  37.7 1.2 collective-permute-start.2
  38.9 4.5 %hidden_tables.1 = (bf16[512,512]{1,0:T(8,128)(2,1)S(1)}, bf16[512,512]{1,0:T(8,128)(2,1)S(1)}) custom-call(), custom_call_target="tpu_custom_call" | custom-call | tf_op jit(solution)/shard_map/hidden_tables/pallas_call | solution.py:85
  43.4 0.0 copy-done.3
  43.4 0.1 reshape.34.refs_3_.refs_2_
  43.5 1.5 %collective-permute-done.refs_0_ = bf16[256,256]{1,0:T(8,128)(2,1)S(1)} collective-permute-done((bf16[256,256]{1,0:T(8,128)(2,1)S(1)}, bf16[256,256]{1,0:T(8,128)(2,1)S(1)}, u32[]{:S(2)}, u32[]{:S(2)}) %collective-permute-start) | collective-permute-done | bytes 131104 | tf_op jit(solution)/shard_map/ppermute | solution.py:458
  45.0 0.0 copy-start
  45.0 3.0 %collective-permute-done.1.refs_1_ = bf16[256,256]{1,0:T(8,128)(2,1)S(1)} collective-permute-done((bf16[256,256]{1,0:T(8,128)(2,1)S(1)}, bf16[256,256]{1,0:T(8,128)(2,1)S(1)}, u32[]{:S(2)}, u32[]{:S(2)}) %collective-permute-start.1) | collective-permute-done | bytes 131104 | tf_op jit(solution)/shard_map/ppermute | solution.py:458
  48.0 0.0 copy-start.1
  48.0 0.0 collective-permute-done.2.refs_2_
  48.0 0.0 copy-start.2
  48.0 0.7 all-to-all-done.1.r_ref
  48.7 0.0 copy-done
  48.7 0.0 copy-done.1
  48.7 0.0 copy-done.2
  48.7 2.7 %mix_rows.1 = (bf16[256,1024]{1,0:T(8,128)(2,1)S(1)}, bf16[768,1024]{1,0:T(8,128)(2,1)S(1)}) custom-call(s32[1]{0:T(128)} %bitcast.chan_ref, bf16[128,8,256]{2,1,0:T(8,128)(2,1)S(1)} %all-to-all-done.1.r_ref, bf16[4,256,256]{2,1,0:T(8,128)(2,1)} %tok_hbm.3, bf16[256,256]{1,0:T(8,128)(2,1)} %copy-done, bf16[256,256]{1,0:T(8,128)(2,1)} %copy-done.1, ...), custom_call_target="tpu_custom_call" | custom-call | tf_op jit(solution)/shard_map/mix_rows/pallas_call | solution.py:350
  51.4 31.1 %all_to_all.20 = bf16[32,24,1024]{2,1,0:T(8,128)(2,1)S(1)} all-to-all(bf16[32,24,1024]{2,1,0:T(8,128)(2,1)S(1)} %bitcast.13), channel_id=1, replica_groups=mesh['seq_0'=4,'seq_1'=4,'seq_2'=2,'chan'=4] {'seq_0','seq_1','seq_2'}, dimensions={0} | all-to-all | bytes 3145728 | tf_op jit(solution)/shard_map/all_to_all | solution.py:440
  82.4 17.2 %expert_rows.1 = bf16[768,1024]{1,0:T(8,128)(2,1)S(1)} custom-call(bf16[768,1024]{1,0:T(8,128)(2,1)S(1)} %bitcast.11, bf16[1,1024,4096]{2,1,0:T(8,128)(2,1)} %wi_hbm.1, bf16[1,4096,1024]{2,1,0:T(8,128)(2,1)} %wo_hbm.1), custom_call_target="tpu_custom_call" | custom-call | tf_op jit(solution)/shard_map/expert_rows/pallas_call | solution.py:406
  99.6 26.2 %all_to_all.21 = bf16[32,24,1024]{2,1,0:T(8,128)(2,1)S(1)} all-to-all(bf16[32,24,1024]{2,1,0:T(8,128)(2,1)S(1)} %bitcast.12), channel_id=1, replica_groups=mesh['seq_0'=4,'seq_1'=4,'seq_2'=2,'chan'=4] {'seq_0','seq_1','seq_2'}, dimensions={0} | all-to-all | bytes 3145728 | tf_op jit(solution)/shard_map/all_to_all | solution.py:440
  125.8 1.8 %finish_rows.1 = bf16[256,1024]{1,0:T(8,128)(2,1)} custom-call(bf16[768,1024]{1,0:T(8,128)(2,1)S(1)} %bitcast.10, bf16[256,1024]{1,0:T(8,128)(2,1)S(1)} %get-tuple-element.29.refs_1_, s32[1,256]{1,0:T(1,128)S(1)} %reshape.34.refs_3_.refs_2_, f32[1,1024]{1,0:T(1,128)S(1)} %get-tuple-element.30.refs_3_), custom_call_target="tpu_custom_call" | custom-call | tf_op jit(solution)/shard_map/finish_rows/pallas_call | solution.py:431
Async XLA Ops:
  2.8 25.6 %all-to-all-start = ((bf16[128,8,256]{2,1,0:T(8,128)(2,1)}), bf16[128,8,256]{2,1,0:T(8,128)(2,1)S(1)}, u32[]{:S(2)}, u32[]{:S(2)}) async-start(bf16[128,8,256]{2,1,0:T(8,128)(2,1)} %get-tuple-element.18), calls=%async_computation | async-start | bytes 1048576 | tf_op jit(solution)/shard_map/all_to_all | solution.py:440
  14.3 29.1 %copy-start.3 = (s32[64,4]{0,1:T(4,128)S(1)}, s32[64,4]{0,1:T(4,128)}, u32[]{:S(2)}) copy-start(s32[64,4]{0,1:T(4,128)} %param.10) | copy-start | bytes 3076
  30.3 18.4 %all-to-all-start.1 = ((bf16[128,8,256]{2,1,0:T(8,128)(2,1)}), bf16[128,8,256]{2,1,0:T(8,128)(2,1)S(1)}, u32[]{:S(2)}, u32[]{:S(2)}) async-start(bf16[128,8,256]{2,1,0:T(8,128)(2,1)} %sequence_sums.1), calls=%async_computation.1 | async-start | bytes 1048576 | tf_op jit(solution)/shard_map/all_to_all | solution.py:440
  33.9 11.1 %collective-permute-start = (bf16[256,256]{1,0:T(8,128)(2,1)S(1)}, bf16[256,256]{1,0:T(8,128)(2,1)S(1)}, u32[]{:S(2)}, u32[]{:S(2)}) collective-permute-start(bf16[256,256]{1,0:T(8,128)(2,1)S(1)} %get-tuple-element.22), channel_id=1, source_target_pairs={{0,1},{1,2},{2,3},{3,0},{4,5},{5,6},{6,7},{7,4},{8,9},{9,10},{10,1... | collective-permute-start | bytes 393224 | tf_op jit(solution)/shard_map/ppermute | solution.py:458
  35.3 12.7 %collective-permute-start.1 = (bf16[256,256]{1,0:T(8,128)(2,1)S(1)}, bf16[256,256]{1,0:T(8,128)(2,1)S(1)}, u32[]{:S(2)}, u32[]{:S(2)}) collective-permute-start(bf16[256,256]{1,0:T(8,128)(2,1)S(1)} %get-tuple-element.23), channel_id=1, source_target_pairs={{0,2},{1,3},{2,0},{3,1},{4,6},{5,7},{6,4},{7,5},{8,10},{9,11},{10,... | collective-permute-start | bytes 393224 | tf_op jit(solution)/shard_map/ppermute | solution.py:458
  37.7 10.3 %collective-permute-start.2 = (bf16[256,256]{1,0:T(8,128)(2,1)S(1)}, bf16[256,256]{1,0:T(8,128)(2,1)S(1)}, u32[]{:S(2)}, u32[]{:S(2)}) collective-permute-start(bf16[256,256]{1,0:T(8,128)(2,1)S(1)} %get-tuple-element.24), channel_id=1, source_target_pairs={{0,3},{1,0},{2,1},{3,2},{4,7},{5,4},{6,5},{7,6},{8,11},{9,8},{10,9... | collective-permute-start | bytes 393224 | tf_op jit(solution)/shard_map/ppermute | solution.py:458
  45.0 3.7 %copy-start = (bf16[256,256]{1,0:T(8,128)(2,1)}, bf16[256,256]{1,0:T(8,128)(2,1)S(1)}, u32[]{:S(2)}) copy-start(bf16[256,256]{1,0:T(8,128)(2,1)S(1)} %collective-permute-done.refs_0_) | copy-start | bytes 393220
  48.0 0.7 copy-start.1
  48.0 0.7 copy-start.2

commit v5 on v4

--- a/solution.py
+++ b/solution.py
@@ -25,7 +25,7 @@
 CH_OWN = CH // N_ALL
 LANES = N_SEQ * DOCS * CH_OWN
 PARTS = 8
-CHUNKS = ((0, 24),)
+SLOTS = 24
 F32 = jnp.float32
 BF16 = jnp.bfloat16
 NN = (((1,), (0,)), ((), ()))
@@ -66,7 +66,20 @@
     ).astype(BF16)
 
 
-def tables_kernel(tc_ref, ts_ref):
+def slot_map(ids):
+    one = (lax.broadcasted_iota(jnp.int32, (N_SEQ, ROWS), 0) == ids).astype(F32)
+    earlier = (
+        lax.broadcasted_iota(jnp.int32, (ROWS, ROWS), 0)
+        < lax.broadcasted_iota(jnp.int32, (ROWS, ROWS), 1)
+    ).astype(BF16)
+    before = mm(one.astype(BF16), earlier, NN)
+    rank = jnp.sum(before * one, axis=0, keepdims=True).astype(jnp.int32)
+    slots = lax.broadcasted_iota(jnp.int32, (N_SEQ * SLOTS, ROWS), 0)
+    return (slots == ids * SLOTS + rank).astype(BF16)
+
+
+def tables_kernel(ids_ref, tc_ref, ts_ref, map_ref):
+    map_ref[...] = slot_map(ids_ref[...])
     block = 128
     f = lax.broadcasted_iota(jnp.int32, (block, D // 2), 1)
     for i in range(D // 2 // block):
@@ -81,17 +94,22 @@
         ts_ref[rows, :] = (-jnp.sin(angle) * factor).astype(BF16)
 
 
-def hidden_tables():
+def make_tables(ids):
     return pl.pallas_call(
         tables_kernel,
-        out_shape=(jax.ShapeDtypeStruct((D // 2, D // 2), BF16),) * 2,
+        out_shape=(
+            jax.ShapeDtypeStruct((D // 2, D // 2), BF16),
+            jax.ShapeDtypeStruct((D // 2, D // 2), BF16),
+            jax.ShapeDtypeStruct((N_SEQ * SLOTS, ROWS), BF16),
+        ),
         compiler_params=kernel_params(8),
-        name="hidden_tables",
-    )()
-
-
-def split_kernel(chan_ref, tok_hbm, col_ref, *refs):
+        name="make_tables",
+    )(ids)
+
+
+def split_kernel(tok_hbm, col_ref, *refs):
     *row_refs, tok_ref, s_ref, sem = refs
+    chan = lax.axis_index("chan")
     moves = [
         pltpu.make_async_copy(tok_hbm.at[doc], tok_ref.at[doc], sem.at[doc]) for doc in range(DOCS)
     ]
@@ -99,7 +117,7 @@
         move.start()
     row = lax.broadcasted_iota(jnp.int32, (CH, CH), 0)
     index = CH_OWN * (row % N_ALL) + row // N_ALL
-    index = jnp.where(chan_ref[0] < N_CHAN // 2, index, (CH - index) % CH)
+    index = jnp.where(chan < N_CHAN // 2, index, (CH - index) % CH)
     pick = (lax.broadcasted_iota(jnp.int32, (CH, CH), 1) == index).astype(BF16)
     for doc in range(DOCS):
         moves[doc].wait()
@@ -114,24 +132,21 @@
             s_ref[h].reshape(N_ALL, PARTS, 128).astype(BF16)
         )
     for i, row_ref in enumerate(row_refs):
-        first = pl.multiple_of((chan_ref[0] + i + 1) % N_CHAN * QUARTER, QUARTER)
+        first = pl.multiple_of((chan + i + 1) % N_CHAN * QUARTER, QUARTER)
         for doc in range(DOCS):
             row_ref[doc * QUARTER : (doc + 1) * QUARTER, :] = tok_ref[
                 doc, pl.ds(first, QUARTER), :
             ]
 
 
-def split_tokens(chan_pos, tokens):
+def split_tokens(tokens):
     cols, *rows = pl.pallas_call(
         split_kernel,
         out_shape=(
             jax.ShapeDtypeStruct((N_ALL, PARTS, POS), BF16),
             *(jax.ShapeDtypeStruct((ROWS, CH), BF16) for _ in range(N_CHAN - 1)),
         ),
-        in_specs=[
-            pl.BlockSpec(memory_space=pltpu.SMEM),
-            pl.BlockSpec(memory_space=pltpu.HBM),
-        ],
+        in_specs=[pl.BlockSpec(memory_space=pltpu.HBM)],
         scratch_shapes=[
             pltpu.VMEM((DOCS, POS, CH), BF16),
             pltpu.VMEM((POS // 128, N_ALL * PARTS, 128), F32),
@@ -139,7 +154,7 @@
         ],
         compiler_params=kernel_params(8),
         name="split_tokens",
-    )(chan_pos, in_hbm(tokens))
+    )(in_hbm(tokens))
     return cols, rows
 
 
@@ -192,10 +207,10 @@
     return out
 
 
-def sequence_kernel(owner_ref, x_ref, twr_ref, twi_ref, tab_ref, out_ref, t_ref, s_ref):
+def sequence_kernel(x_ref, twr_ref, twi_ref, tab_ref, out_ref, t_ref, s_ref):
     rows = DOCS * CH_OWN
     own_mirror = (lax.broadcasted_iota(jnp.int32, (rows, 128), 0) % CH_OWN == 0) & (
-        owner_ref[0] == 0
+        lax.axis_index(SEQ_CHAN) == 0
     )
 
     def folded(g, s, lanes):
@@ -244,19 +259,17 @@
         )
 
 
-def sequence_sums(owner, cols, twr, twi, tab):
+def sequence_sums(cols, twr, twi, tab):
     return pl.pallas_call(
         sequence_kernel,
         out_shape=jax.ShapeDtypeStruct((N_ALL, PARTS, LANES), BF16),
-        in_specs=[pl.BlockSpec(memory_space=pltpu.SMEM)]
-        + [pl.BlockSpec(memory_space=pltpu.VMEM)] * 4,
         scratch_shapes=[
             pltpu.VMEM((4, LANES, 2 * POS), F32),
             pltpu.VMEM((LANES // 128, N_ALL * PARTS, 128), F32),
         ],
         compiler_params=kernel_params(24),
         name="sequence_sums",
-    )(owner, cols, twr, twi, tab)
+    )(cols, twr, twi, tab)
 
 
 def norm_rows(values, gain):
@@ -265,27 +278,10 @@
     return center * lax.rsqrt(spread + 1e-05) * gain
 
 
-def slot_maps(ids):
-    one = (lax.broadcasted_iota(jnp.int32, (N_SEQ, ROWS), 0) == ids).astype(F32)
-    earlier = (
-        lax.broadcasted_iota(jnp.int32, (ROWS, ROWS), 0)
-        < lax.broadcasted_iota(jnp.int32, (ROWS, ROWS), 1)
-    ).astype(BF16)
-    before = mm(one.astype(BF16), earlier, NN)
-    rank = jnp.sum(before * one, axis=0, keepdims=True).astype(jnp.int32)
-    maps = []
-    for start, count in CHUNKS:
-        inside = (rank >= start) & (rank < start + count)
-        target = jnp.where(inside, ids * count + rank - start, -1)
-        slots = lax.broadcasted_iota(jnp.int32, (N_SEQ * count, ROWS), 0)
-        maps.append((slots == target).astype(BF16))
-    return maps
-
-
-def mix_kernel(chan_ref, r_ref, tok_hbm, *refs):
+def mix_kernel(r_ref, tok_hbm, *refs):
     res_refs, rest = refs[: N_CHAN - 1], refs[N_CHAN - 1 :]
-    ids_ref, tc_ref, ts_ref, gain_ref, normed_ref, *out_refs, s_ref, a_ref, x_ref, sem = rest
-    chan = chan_ref[0]
+    slot_ref, tc_ref, ts_ref, gain_ref, normed_ref, out_ref, s_ref, a_ref, x_ref, sem = rest
+    chan = lax.axis_index("chan")
     first = pl.multiple_of(chan * QUARTER, QUARTER)
     moves = [
         pltpu.make_async_copy(
@@ -342,16 +338,15 @@
     residual = jnp.concatenate([x_ref[c].astype(F32) for c in range(N_CHAN)], axis=1)
     normed = norm_rows(residual + mixing, gain_ref[...]).astype(BF16)
     normed_ref[...] = normed
-    for out_ref, chunk in zip(out_refs, slot_maps(ids_ref[...])):
-        out_ref[...] = mm(chunk, normed, NN).astype(BF16)
-
-
-def mix_rows(chan_pos, parts, tokens, residual, ids, tc, ts, gain):
+    out_ref[...] = mm(slot_ref[...], normed, NN).astype(BF16)
+
+
+def mix_rows(parts, tokens, residual, slot, tc, ts, gain):
     return pl.pallas_call(
         mix_kernel,
         out_shape=(
             jax.ShapeDtypeStruct((ROWS, D), BF16),
-            *(jax.ShapeDtypeStruct((N_SEQ * count, D), BF16) for _, count in CHUNKS),
+            jax.ShapeDtypeStruct((N_SEQ * SLOTS, D), BF16),
         ),
         scratch_shapes=[
             pltpu.VMEM((LANES // 128, N_ALL * PARTS, 128), F32),
@@ -359,12 +354,12 @@
             pltpu.VMEM((N_CHAN, ROWS, CH), BF16),
             pltpu.SemaphoreType.DMA((N_CHAN - 1 + DOCS,)),
         ],
-        in_specs=[pl.BlockSpec(memory_space=pltpu.SMEM), pl.BlockSpec(memory_space=pltpu.VMEM)]
+        in_specs=[pl.BlockSpec(memory_space=pltpu.VMEM)]
         + [pl.BlockSpec(memory_space=pltpu.HBM)] * N_CHAN
         + [pl.BlockSpec(memory_space=pltpu.VMEM)] * 4,
         compiler_params=kernel_params(24),
         name="mix_rows",
-    )(chan_pos, parts, *map(in_hbm, (tokens, *residual)), ids, tc, ts, gain)
+    )(parts, *map(in_hbm, (tokens, *residual)), slot, tc, ts, gain)
 
 
 def gelu(v):
@@ -419,21 +414,28 @@
     )(x, in_hbm(expert_in), in_hbm(expert_out))
 
 
-def finish_kernel(*refs):
-    *back_refs, normed_ref, ids_ref, gain_ref, out_ref = refs
-    values = normed_ref[...].astype(F32)
-    for back_ref, chunk in zip(back_refs, slot_maps(ids_ref[...])):
-        values = values + mm(chunk, back_ref[...], TN)
-    out_ref[...] = norm_rows(values, gain_ref[...]).astype(BF16)
-
-
-def finish_rows(back, normed, ids, gain):
+def finish_kernel(back_ref, normed_ref, slot_ref, gain_ref, out_hbm, out_ref, sem):
+    half = ROWS // 2
+    moves = []
+    for i in range(2):
+        rows = slice(i * half, (i + 1) * half)
+        values = normed_ref[rows, :].astype(F32) + mm(slot_ref[:, rows], back_ref[...], TN)
+        out_ref[rows, :] = norm_rows(values, gain_ref[...]).astype(BF16)
+        moves.append(pltpu.make_async_copy(out_ref.at[rows], out_hbm.at[rows], sem.at[i]))
+        moves[i].start()
+    for move in moves:
+        move.wait()
+
+
+def finish_rows(back, normed, slot, gain):
     return pl.pallas_call(
         finish_kernel,
         out_shape=jax.ShapeDtypeStruct((ROWS, D), BF16),
+        out_specs=pl.BlockSpec(memory_space=pltpu.HBM),
+        scratch_shapes=[pltpu.VMEM((ROWS, D), BF16), pltpu.SemaphoreType.DMA((2,))],
         compiler_params=kernel_params(24),
         name="finish_rows",
-    )(*back, normed, ids, gain)
+    )(back, normed, slot, gain)
 
 
 def exchange(x, axes):
@@ -442,27 +444,24 @@
 
 def local(tokens, routing, expert_in, expert_out, gain_mix, gain_out):
     ids = routing.T.reshape(1, ROWS)
-    chan_pos = lax.axis_index("chan").reshape(1)
-    owner = lax.axis_index(SEQ_CHAN).reshape(1)
-    cols, rows = split_tokens(chan_pos, tokens)
+    cols, rows = split_tokens(tokens)
     tables = [jnp.asarray(t) for t in (*twiddle_tables(), position_table())]
     twr, twi, tab, gain_mix, gain_out = bring(
         *tables, gain_mix.reshape(1, D), gain_out.reshape(1, D)
     )
-    tc, ts = hidden_tables()
-    sums = sequence_sums(owner, exchange(cols, SEQ_CHAN), twr, twi, tab)
+    tc, ts, slot = make_tables(ids)
+    sums = sequence_sums(exchange(cols, SEQ_CHAN), twr, twi, tab)
     parts = exchange(sums, SEQ_CHAN)
     residual = []
     for i in range(1, N_CHAN):
         ring = [(c, (c + i) % N_CHAN) for c in range(N_CHAN)]
         residual.append(lax.ppermute(rows[i - 1], "chan", ring))
-    normed, *outgoing = mix_rows(chan_pos, parts, tokens, residual, ids, tc, ts, gain_mix)
-    back = []
-    for (_, count), x in zip(CHUNKS, outgoing):
-        x = exchange(x.reshape(N_SEQ, count, D), SEQ).reshape(N_SEQ * count, D)
-        x = expert_rows(x, expert_in, expert_out)
-        back.append(exchange(x.reshape(N_SEQ, count, D), SEQ).reshape(N_SEQ * count, D))
-    return finish_rows(back, normed, ids, gain_out).reshape(DOCS, QUARTER, D)
+    normed, outgoing = mix_rows(parts, tokens, residual, slot, tc, ts, gain_mix)
+    there = exchange(outgoing.reshape(N_SEQ, SLOTS, D), SEQ)
+    result = expert_rows(there.reshape(N_SEQ * SLOTS, D), expert_in, expert_out)
+    back = exchange(result.reshape(N_SEQ, SLOTS, D), SEQ)
+    out = finish_rows(back.reshape(N_SEQ * SLOTS, D), normed, slot, gain_out)
+    return out.reshape(DOCS, QUARTER, D)
 
 
 def solution(mesh):

time: 128 us -> 128 us (level)
  transfers between devices with their start and end apart: 5 -> 5, of which waited for: 4 -> 4; matrix products, arithmetic and copies ran while one was open for 0% -> 0% of each run, Pallas kernels for 4% -> 5%
where the time goes in v5:
time: 128 us
  blocking collectives  57.3 us (45%)
  Pallas kernels  32.1 us (25%)
  starting transfers between devices  20.1 us (16%)
  waiting for transfers between devices  17.8 us (14%)
    all_to_all x2, blocking collectives, exchange(): return lax.all_to_all(x, axes, split_axis=0, concat_axis=0, tiled=True)  57.3 us
    pallas_call x1, Pallas kernels, expert_rows(): pl.pallas_call(expert_kernel, out_shape=jax.ShapeDtypeStruct((rows, D), B...  17.1 us
    all_to_all x2, starting transfers between devices, exchange(): return lax.all_to_all(x, axes, split_axis=0, concat_axis=0, tiled=True)  15.1 us
    all_to_all x2, waiting for transfers between devices, exchange(): return lax.all_to_all(x, axes, split_axis=0, concat_axis=0, tiled=True)  13.6 us
    ppermute x3, starting transfers between devices, local(): residual.append(lax.ppermute(rows[i - 1], 'chan', ring))  5 us
    pallas_call x1, Pallas kernels, make_tables(): pl.pallas_call(tables_kernel, out_shape=(jax.ShapeDtypeStruct((D // 2, D...  4.84 us
    ppermute x3, waiting for transfers between devices, local(): residual.append(lax.ppermute(rows[i - 1], 'chan', ring))  4.17 us
    pallas_call x1, Pallas kernels, split_tokens(): pl.pallas_call(split_kernel, out_shape=(jax.ShapeDtypeStruct((N_ALL, PART...  2.8 us
  transfers between devices with their start and end apart: 5, of which 4 were waited for; matrix products, arithmetic and copies ran while one was open for 0% of the time, Pallas kernels for 5%

profile of v5, /device:TPU:1, one launch (start us, length us, event | category | flops | bytes accessed | tf_op | source)
XLA Modules:
  0.0 127.6 jit_solution(12893848343136216574)
XLA Ops:
  0.0 2.8 %split_tokens.1 = (bf16[128,8,256]{2,1,0:T(8,128)(2,1)}, bf16[256,256]{1,0:T(8,128)(2,1)S(1)}, bf16[256,256]{1,0:T(8,128)(2,1)S(1)}, bf16[256,256]{1,0:T(8,128)(2,1)S(1)}) custom-call(bf16[4,256,256]{2,1,0:T(8,128)(2,1)} %tok_hbm.3), custom_call_target="tpu_custom_call" | custom-call | tf_op jit(solution)/shard_map/split_tokens/pallas_call | solution.py:143
  2.8 11.5 %all-to-all-start = ((bf16[128,8,256]{2,1,0:T(8,128)(2,1)}), bf16[128,8,256]{2,1,0:T(8,128)(2,1)S(1)}, u32[]{:S(2)}, u32[]{:S(2)}) async-start(bf16[128,8,256]{2,1,0:T(8,128)(2,1)} %get-tuple-element.19), calls=%async_computation | async-start | bytes 1048576 | tf_op jit(solution)/shard_map/all_to_all | solution.py:442
  14.3 0.0 copy-start.3
  14.3 1.1 bring.1
  15.5 13.0 %all-to-all-done.x_ref = bf16[128,8,256]{2,1,0:T(8,128)(2,1)S(1)} async-done(((bf16[128,8,256]{2,1,0:T(8,128)(2,1)}), bf16[128,8,256]{2,1,0:T(8,128)(2,1)S(1)}, u32[]{:S(2)}, u32[]{:S(2)}) %all-to-all-start) | async-done | bytes 524320 | tf_op jit(solution)/shard_map/all_to_all | solution.py:442
  28.4 1.9 %sequence_sums.1 = bf16[128,8,256]{2,1,0:T(8,128)(2,1)} custom-call(bf16[128,8,256]{2,1,0:T(8,128)(2,1)S(1)} %all-to-all-done.x_ref, f32[32,256]{1,0:T(8,128)S(1)} %get-tuple-element.20.twr_ref, f32[32,256]{1,0:T(8,128)S(1)} %get-tuple-element.21.twi_ref, bf16[512,512]{1,0:T(8,128)(2,1)S(1)} %get-tuple-element.22.tab_ref), custom_call_target="tpu_custom_call" | custom-call | tf_op jit(solution)/shard_map/sequence_sums/pallas_call | solution.py:263
  30.3 3.6 %all-to-all-start.1 = ((bf16[128,8,256]{2,1,0:T(8,128)(2,1)}), bf16[128,8,256]{2,1,0:T(8,128)(2,1)S(1)}, u32[]{:S(2)}, u32[]{:S(2)}) async-start(bf16[128,8,256]{2,1,0:T(8,128)(2,1)} %sequence_sums.1), calls=%async_computation.1 | async-start | bytes 1048576 | tf_op jit(solution)/shard_map/all_to_all | solution.py:442
  33.9 1.4 %collective-permute-start = (bf16[256,256]{1,0:T(8,128)(2,1)S(1)}, bf16[256,256]{1,0:T(8,128)(2,1)S(1)}, u32[]{:S(2)}, u32[]{:S(2)}) collective-permute-start(bf16[256,256]{1,0:T(8,128)(2,1)S(1)} %get-tuple-element.23), channel_id=1, source_target_pairs={{0,1},{1,2},{2,3},{3,0},{4,5},{5,6},{6,7},{7,4},{8,9},{9,10},{10,1... | collective-permute-start | bytes 393224 | tf_op jit(solution)/shard_map/ppermute | solution.py:458
  35.4 2.4 %collective-permute-start.1 = (bf16[256,256]{1,0:T(8,128)(2,1)S(1)}, bf16[256,256]{1,0:T(8,128)(2,1)S(1)}, u32[]{:S(2)}, u32[]{:S(2)}) collective-permute-start(bf16[256,256]{1,0:T(8,128)(2,1)S(1)} %get-tuple-element.24), channel_id=1, source_target_pairs={{0,2},{1,3},{2,0},{3,1},{4,6},{5,7},{6,4},{7,5},{8,10},{9,11},{10,... | collective-permute-start | bytes 393224 | tf_op jit(solution)/shard_map/ppermute | solution.py:458
  37.8 1.2 collective-permute-start.2
  38.9 0.0 copy-done.3
  38.9 0.1 reshape.26.ids_ref
  39.0 4.8 %make_tables.1 = (bf16[512,512]{1,0:T(8,128)(2,1)S(1)}, bf16[512,512]{1,0:T(8,128)(2,1)S(1)}, bf16[768,256]{1,0:T(8,128)(2,1)S(1)}) custom-call(s32[1,256]{1,0:T(1,128)S(1)} %reshape.26.ids_ref), custom_call_target="tpu_custom_call" | custom-call | tf_op jit(solution)/shard_map/make_tables/pallas_call | solution.py:98
  43.9 1.2 collective-permute-done.refs_0_
  45.0 0.0 copy-start
  45.0 3.0 %collective-permute-done.1.refs_1_ = bf16[256,256]{1,0:T(8,128)(2,1)S(1)} collective-permute-done((bf16[256,256]{1,0:T(8,128)(2,1)S(1)}, bf16[256,256]{1,0:T(8,128)(2,1)S(1)}, u32[]{:S(2)}, u32[]{:S(2)}) %collective-permute-start.1) | collective-permute-done | bytes 131104 | tf_op jit(solution)/shard_map/ppermute | solution.py:458
  48.0 0.0 copy-start.1
  48.0 0.0 collective-permute-done.2.refs_2_
  48.0 0.0 copy-start.2
  48.0 0.7 all-to-all-done.1.r_ref
  48.7 0.0 copy-done
  48.7 0.0 copy-done.1
  48.7 0.0 copy-done.2
  48.7 2.7 %mix_rows.1 = (bf16[256,1024]{1,0:T(8,128)(2,1)S(1)}, bf16[768,1024]{1,0:T(8,128)(2,1)S(1)}) custom-call(bf16[128,8,256]{2,1,0:T(8,128)(2,1)S(1)} %all-to-all-done.1.r_ref, bf16[4,256,256]{2,1,0:T(8,128)(2,1)} %tok_hbm.3, bf16[256,256]{1,0:T(8,128)(2,1)} %copy-done, bf16[256,256]{1,0:T(8,128)(2,1)} %copy-done.1, bf16[256,256]{1,0:T(8,128)(2,1)} %copy-done.2, ...), custom_call_target="tpu_custom_call" | custom-call | tf_op jit(solution)/shard_map/mix_rows/pallas_call | solution.py:345
  51.4 31.0 %all_to_all.20 = bf16[32,24,1024]{2,1,0:T(8,128)(2,1)S(1)} all-to-all(bf16[32,24,1024]{2,1,0:T(8,128)(2,1)S(1)} %bitcast.11), channel_id=1, replica_groups=mesh['seq_0'=4,'seq_1'=4,'seq_2'=2,'chan'=4] {'seq_0','seq_1','seq_2'}, dimensions={0} | all-to-all | bytes 3145728 | tf_op jit(solution)/shard_map/all_to_all | solution.py:442
  82.4 17.1 %expert_rows.1 = bf16[768,1024]{1,0:T(8,128)(2,1)S(1)} custom-call(bf16[768,1024]{1,0:T(8,128)(2,1)S(1)} %bitcast.9, bf16[1,1024,4096]{2,1,0:T(8,128)(2,1)} %wi_hbm.1, bf16[1,4096,1024]{2,1,0:T(8,128)(2,1)} %wo_hbm.1), custom_call_target="tpu_custom_call" | custom-call | tf_op jit(solution)/shard_map/expert_rows/pallas_call | solution.py:401
  99.6 26.3 %all_to_all.21 = bf16[32,24,1024]{2,1,0:T(8,128)(2,1)S(1)} all-to-all(bf16[32,24,1024]{2,1,0:T(8,128)(2,1)S(1)} %bitcast.10), channel_id=1, replica_groups=mesh['seq_0'=4,'seq_1'=4,'seq_2'=2,'chan'=4] {'seq_0','seq_1','seq_2'}, dimensions={0} | all-to-all | bytes 3145728 | tf_op jit(solution)/shard_map/all_to_all | solution.py:442
  125.8 1.6 %finish_rows.1 = bf16[256,1024]{1,0:T(8,128)(2,1)} custom-call(bf16[768,1024]{1,0:T(8,128)(2,1)S(1)} %bitcast.8, bf16[256,1024]{1,0:T(8,128)(2,1)S(1)} %get-tuple-element.31.normed_ref, bf16[768,256]{1,0:T(8,128)(2,1)S(1)} %get-tuple-element.26.refs_3_.slot_ref, f32[1,1024]{1,0:T(1,128)S(1)} %get-tuple-element.32.gain_ref), custom_call_target="tpu_custom_call" | custom-call | tf_op jit(solution)/shard_map/finish_rows/pallas_call | solution.py:431
Async XLA Ops:
  2.8 25.6 %all-to-all-start = ((bf16[128,8,256]{2,1,0:T(8,128)(2,1)}), bf16[128,8,256]{2,1,0:T(8,128)(2,1)S(1)}, u32[]{:S(2)}, u32[]{:S(2)}) async-start(bf16[128,8,256]{2,1,0:T(8,128)(2,1)} %get-tuple-element.19), calls=%async_computation | async-start | bytes 1048576 | tf_op jit(solution)/shard_map/all_to_all | solution.py:442
  14.3 24.6 %copy-start.3 = (s32[64,4]{0,1:T(4,128)S(1)}, s32[64,4]{0,1:T(4,128)}, u32[]{:S(2)}) copy-start(s32[64,4]{0,1:T(4,128)} %param.10) | copy-start | bytes 3076
  30.3 18.4 %all-to-all-start.1 = ((bf16[128,8,256]{2,1,0:T(8,128)(2,1)}), bf16[128,8,256]{2,1,0:T(8,128)(2,1)S(1)}, u32[]{:S(2)}, u32[]{:S(2)}) async-start(bf16[128,8,256]{2,1,0:T(8,128)(2,1)} %sequence_sums.1), calls=%async_computation.1 | async-start | bytes 1048576 | tf_op jit(solution)/shard_map/all_to_all | solution.py:442
  33.9 11.1 %collective-permute-start = (bf16[256,256]{1,0:T(8,128)(2,1)S(1)}, bf16[256,256]{1,0:T(8,128)(2,1)S(1)}, u32[]{:S(2)}, u32[]{:S(2)}) collective-permute-start(bf16[256,256]{1,0:T(8,128)(2,1)S(1)} %get-tuple-element.23), channel_id=1, source_target_pairs={{0,1},{1,2},{2,3},{3,0},{4,5},{5,6},{6,7},{7,4},{8,9},{9,10},{10,1... | collective-permute-start | bytes 393224 | tf_op jit(solution)/shard_map/ppermute | solution.py:458
  35.4 12.7 %collective-permute-start.1 = (bf16[256,256]{1,0:T(8,128)(2,1)S(1)}, bf16[256,256]{1,0:T(8,128)(2,1)S(1)}, u32[]{:S(2)}, u32[]{:S(2)}) collective-permute-start(bf16[256,256]{1,0:T(8,128)(2,1)S(1)} %get-tuple-element.24), channel_id=1, source_target_pairs={{0,2},{1,3},{2,0},{3,1},{4,6},{5,7},{6,4},{7,5},{8,10},{9,11},{10,... | collective-permute-start | bytes 393224 | tf_op jit(solution)/shard_map/ppermute | solution.py:458
  37.8 10.3 %collective-permute-start.2 = (bf16[256,256]{1,0:T(8,128)(2,1)S(1)}, bf16[256,256]{1,0:T(8,128)(2,1)S(1)}, u32[]{:S(2)}, u32[]{:S(2)}) collective-permute-start(bf16[256,256]{1,0:T(8,128)(2,1)S(1)} %get-tuple-element.25), channel_id=1, source_target_pairs={{0,3},{1,0},{2,1},{3,2},{4,7},{5,4},{6,5},{7,6},{8,11},{9,8},{10,9... | collective-permute-start | bytes 393224 | tf_op jit(solution)/shard_map/ppermute | solution.py:458
  45.0 3.7 %copy-start = (bf16[256,256]{1,0:T(8,128)(2,1)}, bf16[256,256]{1,0:T(8,128)(2,1)S(1)}, u32[]{:S(2)}) copy-start(bf16[256,256]{1,0:T(8,128)(2,1)S(1)} %collective-permute-done.refs_0_) | copy-start | bytes 393220
  48.0 0.7 copy-start.1
  48.0 0.7 copy-start.2

commit v6 on v5

--- a/solution.py
+++ b/solution.py
@@ -107,20 +107,13 @@
     )(ids)
 
 
-def split_kernel(tok_hbm, col_ref, *refs):
-    *row_refs, tok_ref, s_ref, sem = refs
+def split_kernel(tok_ref, col_ref, s_ref):
     chan = lax.axis_index("chan")
-    moves = [
-        pltpu.make_async_copy(tok_hbm.at[doc], tok_ref.at[doc], sem.at[doc]) for doc in range(DOCS)
-    ]
-    for move in moves:
-        move.start()
     row = lax.broadcasted_iota(jnp.int32, (CH, CH), 0)
     index = CH_OWN * (row % N_ALL) + row // N_ALL
     index = jnp.where(chan < N_CHAN // 2, index, (CH - index) % CH)
     pick = (lax.broadcasted_iota(jnp.int32, (CH, CH), 1) == index).astype(BF16)
     for doc in range(DOCS):
-        moves[doc].wait()
         flipped = mm(pick, tok_ref[doc], NT)
         for j in range(CH_OWN):
             for h in range(POS // 128):
@@ -131,31 +124,49 @@
         col_ref[:, :, h * 128 : (h + 1) * 128] = (
             s_ref[h].reshape(N_ALL, PARTS, 128).astype(BF16)
         )
-    for i, row_ref in enumerate(row_refs):
-        first = pl.multiple_of((chan + i + 1) % N_CHAN * QUARTER, QUARTER)
-        for doc in range(DOCS):
-            row_ref[doc * QUARTER : (doc + 1) * QUARTER, :] = tok_ref[
-                doc, pl.ds(first, QUARTER), :
-            ]
 
 
 def split_tokens(tokens):
-    cols, *rows = pl.pallas_call(
+    return pl.pallas_call(
         split_kernel,
-        out_shape=(
-            jax.ShapeDtypeStruct((N_ALL, PARTS, POS), BF16),
-            *(jax.ShapeDtypeStruct((ROWS, CH), BF16) for _ in range(N_CHAN - 1)),
-        ),
-        in_specs=[pl.BlockSpec(memory_space=pltpu.HBM)],
+        out_shape=jax.ShapeDtypeStruct((N_ALL, PARTS, POS), BF16),
         scratch_shapes=[
-            pltpu.VMEM((DOCS, POS, CH), BF16),
             pltpu.VMEM((POS // 128, N_ALL * PARTS, 128), F32),
-            pltpu.SemaphoreType.DMA((DOCS,)),
         ],
         compiler_params=kernel_params(8),
         name="split_tokens",
+    )(tokens)
+
+
+def cut_kernel(tok_hbm, *refs):
+    *row_hbms, sem = refs
+    moves = []
+    for i, row_hbm in enumerate(row_hbms):
+        first = pl.multiple_of((lax.axis_index("chan") + i + 1) % N_CHAN * QUARTER, QUARTER)
+        for doc in range(DOCS):
+            moves.append(
+                pltpu.make_async_copy(
+                    tok_hbm.at[doc, pl.ds(first, QUARTER), :],
+                    row_hbm.at[pl.ds(doc * QUARTER, QUARTER), :],
+                    sem.at[len(moves)],
+                )
+            )
+    for move in moves:
+        move.start()
+    for move in moves:
+        move.wait()
+
+
+def cut_rows(tokens):
+    return pl.pallas_call(
+        cut_kernel,
+        out_shape=tuple(jax.ShapeDtypeStruct((ROWS, CH), BF16) for _ in range(N_CHAN - 1)),
+        in_specs=[pl.BlockSpec(memory_space=pltpu.HBM)],
+        out_specs=(pl.BlockSpec(memory_space=pltpu.HBM),) * (N_CHAN - 1),
+        scratch_shapes=[pltpu.SemaphoreType.DMA(((N_CHAN - 1) * DOCS,))],
+        compiler_params=kernel_params(4),
+        name="cut_rows",
     )(in_hbm(tokens))
-    return cols, rows
 
 
 def bring_kernel(*refs):
@@ -369,7 +380,7 @@
 
 def expert_kernel(x_ref, wi_hbm, wo_hbm, out_ref, wi_ref, wo_ref, h_ref, sem):
     ff = wi_ref.shape[1]
-    pieces, block, width = 8, 1024, 256
+    pieces, width = 8, 256
     step = ff // pieces
     moves = [
         pltpu.make_async_copy(
@@ -384,10 +395,10 @@
     ]
     for move in moves:
         move.start()
-    for i in range(ff // block):
-        for j in range(i * block // step, (i + 1) * block // step):
-            moves[j].wait()
-        cols = slice(i * block, (i + 1) * block)
+    for first, count in ((0, 1), (1, 1), (2, 2), (4, 2), (6, 2)):
+        for move in moves[first : first + count]:
+            move.wait()
+        cols = slice(first * step, (first + count) * step)
         h_ref[:, cols] = gelu(mm(x_ref[...], wi_ref[:, cols], NN)).astype(BF16)
     for move in moves[pieces:]:
         move.wait()
@@ -444,7 +455,7 @@
 
 def local(tokens, routing, expert_in, expert_out, gain_mix, gain_out):
     ids = routing.T.reshape(1, ROWS)
-    cols, rows = split_tokens(tokens)
+    cols, rows = split_tokens(tokens), cut_rows(tokens)
     tables = [jnp.asarray(t) for t in (*twiddle_tables(), position_table())]
     twr, twi, tab, gain_mix, gain_out = bring(
         *tables, gain_mix.reshape(1, D), gain_out.reshape(1, D)

time: 128 us -> 127 us (level)
    pallas_call x1 -> x2, Pallas kernels: 2.8 us -> 2.29 us  [the longest x1 1.23 us: split_tokens(): pl.pallas_call(split_kernel, out_shape=jax.ShapeDtypeStruct((N_ALL, PARTS...]
  transfers between devices with their start and end apart: 5 -> 5, of which waited for: 4 -> 4; matrix products, arithmetic and copies ran while one was open for 0% -> 0% of each run, Pallas kernels for 5% -> 6%
where the time goes in v6:
time: 127 us
  blocking collectives  57.3 us (45%)
  Pallas kernels  31.5 us (25%)
  starting transfers between devices  20.1 us (16%)
  waiting for transfers between devices  16.7 us (13%)
    all_to_all x2, blocking collectives, exchange(): return lax.all_to_all(x, axes, split_axis=0, concat_axis=0, tiled=True)  57.3 us
    pallas_call x1, Pallas kernels, expert_rows(): pl.pallas_call(expert_kernel, out_shape=jax.ShapeDtypeStruct((rows, D), B...  17.1 us
    all_to_all x2, starting transfers between devices, exchange(): return lax.all_to_all(x, axes, split_axis=0, concat_axis=0, tiled=True)  15.1 us
    all_to_all x2, waiting for transfers between devices, exchange(): return lax.all_to_all(x, axes, split_axis=0, concat_axis=0, tiled=True)  13.6 us
    ppermute x3, starting transfers between devices, local(): residual.append(lax.ppermute(rows[i - 1], 'chan', ring))  5 us
    pallas_call x1, Pallas kernels, make_tables(): pl.pallas_call(tables_kernel, out_shape=(jax.ShapeDtypeStruct((D // 2, D...  4.84 us
    ppermute x3, waiting for transfers between devices, local(): residual.append(lax.ppermute(rows[i - 1], 'chan', ring))  3.11 us
    pallas_call x1, Pallas kernels, mix_rows(): pl.pallas_call(mix_kernel, out_shape=(jax.ShapeDtypeStruct((ROWS, D), BF1...  2.67 us
  transfers between devices with their start and end apart: 5, of which 4 were waited for; matrix products, arithmetic and copies ran while one was open for 0% of the time, Pallas kernels for 6%

profile of v6, /device:TPU:1, one launch (start us, length us, event | category | flops | bytes accessed | tf_op | source)
XLA Modules:
  0.0 127.0 jit_solution(9705330561536499136)
XLA Ops:
  0.0 0.0 copy-start
  0.0 1.0 copy-done
  1.0 1.2 split_tokens.1
  2.3 11.5 %all-to-all-start = ((bf16[128,8,256]{2,1,0:T(8,128)(2,1)}), bf16[128,8,256]{2,1,0:T(8,128)(2,1)S(1)}, u32[]{:S(2)}, u32[]{:S(2)}) async-start(bf16[128,8,256]{2,1,0:T(8,128)(2,1)} %split_tokens.1), calls=%async_computation | async-start | bytes 1048576 | tf_op jit(solution)/shard_map/all_to_all | solution.py:453
  13.8 1.1 bring.1
  14.9 13.0 %all-to-all-done.x_ref = bf16[128,8,256]{2,1,0:T(8,128)(2,1)S(1)} async-done(((bf16[128,8,256]{2,1,0:T(8,128)(2,1)}), bf16[128,8,256]{2,1,0:T(8,128)(2,1)S(1)}, u32[]{:S(2)}, u32[]{:S(2)}) %all-to-all-start) | async-done | bytes 524320 | tf_op jit(solution)/shard_map/all_to_all | solution.py:453
  27.9 0.0 copy-start.4
  27.9 1.9 %sequence_sums.1 = bf16[128,8,256]{2,1,0:T(8,128)(2,1)} custom-call(bf16[128,8,256]{2,1,0:T(8,128)(2,1)S(1)} %all-to-all-done.x_ref, f32[32,256]{1,0:T(8,128)S(1)} %get-tuple-element.18.twr_ref, f32[32,256]{1,0:T(8,128)S(1)} %get-tuple-element.19.twi_ref, bf16[512,512]{1,0:T(8,128)(2,1)S(1)} %get-tuple-element.20.tab_ref), custom_call_target="tpu_custom_call" | custom-call | tf_op jit(solution)/shard_map/sequence_sums/pallas_call | solution.py:274
  29.8 3.6 %all-to-all-start.1 = ((bf16[128,8,256]{2,1,0:T(8,128)(2,1)}), bf16[128,8,256]{2,1,0:T(8,128)(2,1)S(1)}, u32[]{:S(2)}, u32[]{:S(2)}) async-start(bf16[128,8,256]{2,1,0:T(8,128)(2,1)} %sequence_sums.1), calls=%async_computation.1 | async-start | bytes 1048576 | tf_op jit(solution)/shard_map/all_to_all | solution.py:453
  33.4 1.1 cut_rows.1
  34.5 1.4 %collective-permute-start = (bf16[256,256]{1,0:T(8,128)(2,1)S(1)}, bf16[256,256]{1,0:T(8,128)(2,1)S(1)}, u32[]{:S(2)}, u32[]{:S(2)}) collective-permute-start(bf16[256,256]{1,0:T(8,128)(2,1)S(1)} %get-tuple-element.21), channel_id=1, source_target_pairs={{0,1},{1,2},{2,3},{3,0},{4,5},{5,6},{6,7},{7,4},{8,9},{9,10},{10,1... | collective-permute-start | bytes 393224 | tf_op jit(solution)/shard_map/ppermute | solution.py:469
  35.9 2.4 %collective-permute-start.1 = (bf16[256,256]{1,0:T(8,128)(2,1)S(1)}, bf16[256,256]{1,0:T(8,128)(2,1)S(1)}, u32[]{:S(2)}, u32[]{:S(2)}) collective-permute-start(bf16[256,256]{1,0:T(8,128)(2,1)S(1)} %get-tuple-element.22), channel_id=1, source_target_pairs={{0,2},{1,3},{2,0},{3,1},{4,6},{5,7},{6,4},{7,5},{8,10},{9,11},{10,... | collective-permute-start | bytes 393224 | tf_op jit(solution)/shard_map/ppermute | solution.py:469
  38.3 1.2 collective-permute-start.2
  39.5 0.0 copy-done.4
  39.5 0.1 reshape.26.ids_ref
  39.5 4.8 %make_tables.1 = (bf16[512,512]{1,0:T(8,128)(2,1)S(1)}, bf16[512,512]{1,0:T(8,128)(2,1)S(1)}, bf16[768,256]{1,0:T(8,128)(2,1)S(1)}) custom-call(s32[1,256]{1,0:T(1,128)S(1)} %reshape.26.ids_ref), custom_call_target="tpu_custom_call" | custom-call | tf_op jit(solution)/shard_map/make_tables/pallas_call | solution.py:98
  44.4 0.1 collective-permute-done.refs_0_
  44.5 0.0 copy-start.1
  44.5 3.0 %collective-permute-done.1.refs_1_ = bf16[256,256]{1,0:T(8,128)(2,1)S(1)} collective-permute-done((bf16[256,256]{1,0:T(8,128)(2,1)S(1)}, bf16[256,256]{1,0:T(8,128)(2,1)S(1)}, u32[]{:S(2)}, u32[]{:S(2)}) %collective-permute-start.1) | collective-permute-done | bytes 131104 | tf_op jit(solution)/shard_map/ppermute | solution.py:469
  47.5 0.0 copy-start.2
  47.5 0.0 collective-permute-done.2.refs_2_
  47.5 0.0 copy-start.3
  47.5 0.7 all-to-all-done.1.r_ref
  48.2 0.0 copy-done.1
  48.2 0.0 copy-done.2
  48.2 0.0 copy-done.3
  48.2 2.7 %mix_rows.1 = (bf16[256,1024]{1,0:T(8,128)(2,1)S(1)}, bf16[768,1024]{1,0:T(8,128)(2,1)S(1)}) custom-call(bf16[128,8,256]{2,1,0:T(8,128)(2,1)S(1)} %all-to-all-done.1.r_ref, bf16[4,256,256]{2,1,0:T(8,128)(2,1)} %tok_hbm.3, bf16[256,256]{1,0:T(8,128)(2,1)} %copy-done.1, bf16[256,256]{1,0:T(8,128)(2,1)} %copy-done.2, bf16[256,256]{1,0:T(8,128)(2,1)} %copy-done.3, ...), custom_call_target="tpu_custom_call" | custom-call | tf_op jit(solution)/shard_map/mix_rows/pallas_call | solution.py:356
  50.9 31.0 %all_to_all.20 = bf16[32,24,1024]{2,1,0:T(8,128)(2,1)S(1)} all-to-all(bf16[32,24,1024]{2,1,0:T(8,128)(2,1)S(1)} %bitcast.11), channel_id=1, replica_groups=mesh['seq_0'=4,'seq_1'=4,'seq_2'=2,'chan'=4] {'seq_0','seq_1','seq_2'}, dimensions={0} | all-to-all | bytes 3145728 | tf_op jit(solution)/shard_map/all_to_all | solution.py:453
  81.9 17.1 %expert_rows.1 = bf16[768,1024]{1,0:T(8,128)(2,1)S(1)} custom-call(bf16[768,1024]{1,0:T(8,128)(2,1)S(1)} %bitcast.9, bf16[1,1024,4096]{2,1,0:T(8,128)(2,1)} %wi_hbm.1, bf16[1,4096,1024]{2,1,0:T(8,128)(2,1)} %wo_hbm.1), custom_call_target="tpu_custom_call" | custom-call | tf_op jit(solution)/shard_map/expert_rows/pallas_call | solution.py:412
  99.0 26.2 %all_to_all.21 = bf16[32,24,1024]{2,1,0:T(8,128)(2,1)S(1)} all-to-all(bf16[32,24,1024]{2,1,0:T(8,128)(2,1)S(1)} %bitcast.10), channel_id=1, replica_groups=mesh['seq_0'=4,'seq_1'=4,'seq_2'=2,'chan'=4] {'seq_0','seq_1','seq_2'}, dimensions={0} | all-to-all | bytes 3145728 | tf_op jit(solution)/shard_map/all_to_all | solution.py:453
  125.2 1.6 %finish_rows.1 = bf16[256,1024]{1,0:T(8,128)(2,1)} custom-call(bf16[768,1024]{1,0:T(8,128)(2,1)S(1)} %bitcast.8, bf16[256,1024]{1,0:T(8,128)(2,1)S(1)} %get-tuple-element.29.normed_ref, bf16[768,256]{1,0:T(8,128)(2,1)S(1)} %get-tuple-element.24.refs_3_.slot_ref, f32[1,1024]{1,0:T(1,128)S(1)} %get-tuple-element.30.gain_ref), custom_call_target="tpu_custom_call" | custom-call | tf_op jit(solution)/shard_map/finish_rows/pallas_call | solution.py:442
Async XLA Ops:
  0.0 1.0 copy-start
  2.3 25.6 %all-to-all-start = ((bf16[128,8,256]{2,1,0:T(8,128)(2,1)}), bf16[128,8,256]{2,1,0:T(8,128)(2,1)S(1)}, u32[]{:S(2)}, u32[]{:S(2)}) async-start(bf16[128,8,256]{2,1,0:T(8,128)(2,1)} %split_tokens.1), calls=%async_computation | async-start | bytes 1048576 | tf_op jit(solution)/shard_map/all_to_all | solution.py:453
  27.9 11.6 %copy-start.4 = (s32[64,4]{0,1:T(4,128)S(1)}, s32[64,4]{0,1:T(4,128)}, u32[]{:S(2)}) copy-start(s32[64,4]{0,1:T(4,128)} %param.10) | copy-start | bytes 3076
  29.8 18.4 %all-to-all-start.1 = ((bf16[128,8,256]{2,1,0:T(8,128)(2,1)}), bf16[128,8,256]{2,1,0:T(8,128)(2,1)S(1)}, u32[]{:S(2)}, u32[]{:S(2)}) async-start(bf16[128,8,256]{2,1,0:T(8,128)(2,1)} %sequence_sums.1), calls=%async_computation.1 | async-start | bytes 1048576 | tf_op jit(solution)/shard_map/all_to_all | solution.py:453
  34.5 10.0 %collective-permute-start = (bf16[256,256]{1,0:T(8,128)(2,1)S(1)}, bf16[256,256]{1,0:T(8,128)(2,1)S(1)}, u32[]{:S(2)}, u32[]{:S(2)}) collective-permute-start(bf16[256,256]{1,0:T(8,128)(2,1)S(1)} %get-tuple-element.21), channel_id=1, source_target_pairs={{0,1},{1,2},{2,3},{3,0},{4,5},{5,6},{6,7},{7,4},{8,9},{9,10},{10,1... | collective-permute-start | bytes 393224 | tf_op jit(solution)/shard_map/ppermute | solution.py:469
  35.9 11.6 %collective-permute-start.1 = (bf16[256,256]{1,0:T(8,128)(2,1)S(1)}, bf16[256,256]{1,0:T(8,128)(2,1)S(1)}, u32[]{:S(2)}, u32[]{:S(2)}) collective-permute-start(bf16[256,256]{1,0:T(8,128)(2,1)S(1)} %get-tuple-element.22), channel_id=1, source_target_pairs={{0,2},{1,3},{2,0},{3,1},{4,6},{5,7},{6,4},{7,5},{8,10},{9,11},{10,... | collective-permute-start | bytes 393224 | tf_op jit(solution)/shard_map/ppermute | solution.py:469
  38.3 9.2 %collective-permute-start.2 = (bf16[256,256]{1,0:T(8,128)(2,1)S(1)}, bf16[256,256]{1,0:T(8,128)(2,1)S(1)}, u32[]{:S(2)}, u32[]{:S(2)}) collective-permute-start(bf16[256,256]{1,0:T(8,128)(2,1)S(1)} %get-tuple-element.23), channel_id=1, source_target_pairs={{0,3},{1,0},{2,1},{3,2},{4,7},{5,4},{6,5},{7,6},{8,11},{9,8},{10,9... | collective-permute-start | bytes 393224 | tf_op jit(solution)/shard_map/ppermute | solution.py:469
  44.5 3.7 %copy-start.1 = (bf16[256,256]{1,0:T(8,128)(2,1)}, bf16[256,256]{1,0:T(8,128)(2,1)S(1)}, u32[]{:S(2)}) copy-start(bf16[256,256]{1,0:T(8,128)(2,1)S(1)} %collective-permute-done.refs_0_) | copy-start | bytes 393220
  47.5 0.7 copy-start.2
  47.5 0.7 copy-start.3
